TPU v7x, 32 devices: a whole 2x2x4 slice. The times are simulated.
32 devices in a mesh: pb: 2 (over core), ka: 16 (over z, y, x).
Axes of the slice: x: 2, y: 2, z: 4, core: 2. Of those that a mesh axis runs over, the one named last changes fastest.
Arguments:
- vertex_ladder: float32 [2, 8, 1024, 1024], P(None, 'pb', 'ka'), may hold values from -6 to 6
- vertex_cross_a: float32 [2, 8, 1024, 1024], P(None, 'pb', 'ka'), may hold values from -6 to 6
- vertex_cross_b: float32 [2, 8, 1024, 1024], P(None, 'pb', 'ka'), may hold values from -6 to 6
- bubble: float32 [2, 8, 1024], P(None, 'pb'), may hold values from -0.072 to 0.072
- row_maps: int32 [2, 8, 1024], replicated, may hold values from 0 to 8191, as said below
- col_maps: int32 [2, 1024], replicated, may hold values from 0 to 1023, each once within a row
Outputs:
- ladder_out: float32 [2, 8, 1024, 1024], P(None, 'pb', 'ka')
- crossed_a: float32 [2, 8, 1024, 1024], P(None, 'pb', 'ka')
- crossed_b: float32 [2, 8, 1024, 1024], P(None, 'pb', 'ka')
Inputs may be any that keep to these rules, and one draw needn't show every extreme that they name: `row_maps`: each of the two maps is a permutation of all 8192 rows. A device holds the rows of its bosonic indices (index of pb) and its first fermionic indices (index of ka); the 256 rows of one device take exactly 8 of their source rows from each device.
All inputs are finite; a program needn't handle non-finite values.
Results may differ from a plain program's by a relative error of at most 0.007.
Values may be sent and summed in bfloat16 or wider, within the bound.
No kernel may reach another device: no remote copies, remote signals or barrier semaphores. Data moves between devices by JAX's collectives and lax.ppermute only.
A program may use at most 64 MiB of HBM per device.

v0:
```python
import functools

import jax
import jax.numpy as jnp
from jax import lax
from jax.experimental import pallas as pl
from jax.experimental.pallas import tpu as pltpu
from jax.sharding import PartitionSpec as P


LADDER = 6
TILE = 256


def ladder_kernel(groups, low_count, wanted, place_ref, chi_ref, *refs):
    total = groups * low_count * 2
    pieces = refs[:total]
    outs = refs[total : total + len(wanted)]
    right, left, base, sems = refs[total + len(wanted) :]
    rows = pieces[0].shape[1]
    depth = pieces[0].shape[2]
    count = len(wanted) * rows
    plane = 2 * low_count
    group, low, core = place_ref[0], place_ref[1], place_ref[2]

    def start_of(d, e, c):
        member = lax.bitwise_xor(core, c) * low_count + lax.bitwise_xor(low, e)
        return pl.multiple_of((lax.bitwise_xor(group, d) * plane + member) * rows, rows)

    copies = []
    for d in range(groups):
        for e in range(low_count):
            for c in range(2):
                number = (d * low_count + e) * 2 + c
                for part in range(2):
                    copy = pltpu.make_async_copy(
                        pieces[number].at[part],
                        right.at[pl.ds(part * depth + start_of(d, e, c), rows), :],
                        sems.at[number * 2 + part],
                    )
                    copy.start()
                    copies.append(copy)
    for copy in copies:
        copy.wait()
    for i, d in enumerate(wanted):
        for part in range(2):
            base[pl.ds(part * count + i * rows, rows), :] = right[
                pl.ds(part * depth + start_of(d, 0, 0), rows), :
            ]

    def scaled(slot, columns, real, imag):
        chi_re, chi_im = chi_ref[0:1, columns], chi_ref[1:2, columns]
        scaled_re = real * chi_re - imag * chi_im
        scaled_im = real * chi_im + imag * chi_re
        low_re = scaled_re.astype(jnp.bfloat16)
        low_im = scaled_im.astype(jnp.bfloat16)
        shifted = slice(columns.start + depth, columns.stop + depth)
        left[slot, :count, columns] = low_re
        left[slot, count:, columns] = low_im
        left[slot, count:, shifted] = low_re
        left[slot, :count, shifted] = -low_im

    tiles = [slice(j * TILE, (j + 1) * TILE) for j in range(depth // TILE)]
    for columns in tiles:
        whole = base[:, columns].astype(jnp.float32)
        scaled(0, columns, whole[:count], whole[count:])
    for step in range(LADDER):
        for columns in tiles:
            product = jnp.dot(
                left[step % 2], right[:, columns], preferred_element_type=jnp.float32
            )
            if step < LADDER - 1:
                whole = product + base[:, columns].astype(jnp.float32)
                scaled((step + 1) % 2, columns, whole[:count], whole[count:])
            else:
                rounded = product.astype(jnp.bfloat16)
                for i in range(len(wanted)):
                    for part in range(2):
                        start = part * count + i * rows
                        outs[i][part, :, columns] = rounded[start : start + rows]


def ladder(place, chi, pieces, groups, low_count, wanted):
    _, rows, depth = pieces[0].shape
    count = len(wanted) * rows
    total = groups * low_count * 2
    return pl.pallas_call(
        functools.partial(ladder_kernel, groups, low_count, wanted),
        out_shape=[jax.ShapeDtypeStruct((2, rows, depth), jnp.bfloat16)] * len(wanted),
        in_specs=[
            pl.BlockSpec(memory_space=pltpu.SMEM),
            pl.BlockSpec(memory_space=pltpu.VMEM),
        ]
        + [pl.BlockSpec(memory_space=pl.ANY)] * total,
        out_specs=[pl.BlockSpec(memory_space=pltpu.VMEM)] * len(wanted),
        scratch_shapes=[
            pltpu.VMEM((2 * depth, depth), jnp.bfloat16),
            pltpu.VMEM((2, 2 * count, 2 * depth), jnp.bfloat16),
            pltpu.VMEM((2 * count, depth), jnp.bfloat16),
            pltpu.SemaphoreType.DMA((total * 2,)),
        ],
        cost_estimate=pl.CostEstimate(
            flops=LADDER * 8 * count * depth * depth,
            bytes_accessed=4 * depth * depth + 8 * count * depth,
            transcendentals=0,
        ),
        name="ladder",
    )(place, chi, *pieces)


def select_kernel(chosen_ref, *refs):
    groups = len(refs) - 1
    out = refs[-1]
    depth = refs[0].shape[2]
    for part in range(2):
        rows = jnp.concatenate([refs[d][part] for d in range(groups)], 0)
        out[:, part * depth : (part + 1) * depth] = jnp.dot(
            chosen_ref[...], rows, preferred_element_type=jnp.float32
        ).astype(jnp.bfloat16)


def select_rows(chosen, returned):
    _, _, depth = returned[0].shape
    return pl.pallas_call(
        select_kernel,
        out_shape=jax.ShapeDtypeStruct((chosen.shape[0], 2 * depth), jnp.bfloat16),
        cost_estimate=pl.CostEstimate(
            flops=4 * chosen.shape[0] * chosen.shape[1] * depth,
            bytes_accessed=8 * chosen.shape[0] * depth,
            transcendentals=0,
        ),
        name="select_rows",
    )(chosen, *returned)


def place_kernel(rows_ref, columns_ref, received_ref, base_ref, out_ref):
    picked = jnp.dot(
        rows_ref[...], received_ref[...], preferred_element_type=jnp.float32
    ).astype(jnp.bfloat16)
    out_ref[0] = base_ref[0] + jnp.dot(
        picked, columns_ref[...], preferred_element_type=jnp.float32
    )


def place_rows(row_pick, column_pick, received, base):
    count, slots = row_pick.shape
    depth = column_pick.shape[0]
    return pl.pallas_call(
        place_kernel,
        out_shape=jax.ShapeDtypeStruct((2, count, depth), jnp.float32),
        grid=(2,),
        in_specs=[
            pl.BlockSpec((count, slots), lambda part: (0, 0)),
            pl.BlockSpec((depth, depth), lambda part: (0, 0)),
            pl.BlockSpec((slots, depth), lambda part: (0, part)),
            pl.BlockSpec((1, count, depth), lambda part: (part, 0, 0)),
        ],
        out_specs=pl.BlockSpec((1, count, depth), lambda part: (part, 0, 0)),
        cost_estimate=pl.CostEstimate(
            flops=4 * count * depth * (slots + depth),
            bytes_accessed=16 * count * depth + 2 * depth * depth,
            transcendentals=0,
        ),
        name="place_rows",
    )(row_pick, column_pick, received, base)


def per_device(vertex_ladder, vertex_cross_a, vertex_cross_b, bubble, row_maps, col_maps):
    _, q_local, row_count, col_count = vertex_ladder.shape
    pb_count = lax.axis_size("pb")
    ka_count = lax.axis_size("ka")
    dev_count = pb_count * ka_count
    plane = ka_count // q_local
    low_count = plane // 2
    local_count = q_local * row_count
    per_peer = local_count // dev_count
    my_pb = lax.axis_index("pb")
    my_ka = lax.axis_index("ka")
    group, member = my_ka // plane, my_ka % plane
    core, top, low = my_pb % 2, member // low_count, member % low_count

    def twin_of(index):
        pb, ka = index // ka_count, index % ka_count
        other, upper = pb % 2, ka % plane // low_count
        return (pb - other + upper) * ka_count + ka + (other - upper) * low_count

    my_device = my_pb * ka_count + my_ka
    my_twin = twin_of(my_device)

    def move(value, target):
        return lax.ppermute(value, ("pb", "ka"), [(i, target(i)) for i in range(dev_count)])

    gamma_low = vertex_ladder.astype(jnp.bfloat16)

    def piece_of(index):
        return lax.dynamic_index_in_dim(gamma_low, index, 1, keepdims=False)

    held = {}
    for d in range(q_local):
        held[d, 0, 0] = move(piece_of(group ^ d), lambda i, d=d: twin_of(i) ^ (d * plane))
    bits = [1 << b for b in range(low_count.bit_length() - 1)]
    for d in range(q_local):
        have = [0]
        for bit in bits:
            for e in have:
                held[d, e ^ bit, 0] = move(held[d, e, 0], lambda i, bit=bit: i ^ bit)
            have = have + [e ^ bit for e in have]
        for e in have:
            held[d, e, 1] = move(held[d, e, 0], lambda i: i ^ ka_count)
    pieces = [held[d, e, c] for d in range(q_local) for e in range(low_count) for c in range(2)]
    own_chi = lax.dynamic_index_in_dim(bubble, group, 1, keepdims=False)
    other_chi = move(own_chi, lambda i: i ^ ka_count)
    chi = jnp.where(core == top, own_chi, other_chi)
    place = jnp.stack([group, low, core]).astype(jnp.int32)
    results = {}
    for wanted in parts_of(q_local):
        outs = ladder(place, chi, pieces, q_local, low_count, wanted)
        for d, out in zip(wanted, outs):
            results[d] = out
    returned = [results[0]] + [
        move(results[d], lambda i, d=d: i ^ (d * plane)) for d in range(1, q_local)
    ]

    def device_of(global_rows):
        return global_rows // col_count // q_local * ka_count + global_rows % col_count // row_count

    def chosen_of(by_device):
        mine = (device_of(by_device) == my_twin).astype(jnp.int32)
        rank = jnp.cumsum(mine, 1) - 1
        source_q = by_device // col_count % q_local
        source_place = (source_q ^ group) * row_count + by_device % col_count % row_count
        slot_ids = jnp.arange(per_peer, dtype=jnp.int32)
        hits = mine[:, :, None] * (rank[:, :, None] == slot_ids[None, None, :]).astype(jnp.int32)
        return jnp.sum(hits * source_place[:, :, None], 1)

    def slots_of(by_device):
        source_dev = device_of(
            lax.dynamic_index_in_dim(by_device, my_device, 0, keepdims=False)
        )
        onehot = (source_dev[:, None] == jnp.arange(dev_count, dtype=jnp.int32)[None, :]).astype(
            jnp.int32
        )
        slot_index = jnp.sum((jnp.cumsum(onehot, 0) - onehot) * onehot, 1)
        return twin_of(source_dev), slot_index

    tables = [
        row_maps[channel]
        .reshape(pb_count, q_local, ka_count, row_count)
        .transpose(0, 2, 1, 3)
        .reshape(dev_count, local_count)
        for channel in range(2)
    ]
    chosen = jnp.stack([chosen_of(table) for table in tables], 1).reshape(-1)
    chosen = (chosen[:, None] == jnp.arange(local_count, dtype=jnp.int32)[None, :]).astype(
        jnp.bfloat16
    )
    send = select_rows(chosen, returned)
    received = lax.all_to_all(
        send.reshape(dev_count, 2 * per_peer, 2 * col_count), ("pb", "ka"), 0, 0, tiled=True
    ).reshape(dev_count * 2 * per_peer, 2 * col_count)

    stacked = jnp.stack([move(returned[d], twin_of) for d in range(q_local)])
    order = jnp.arange(q_local, dtype=jnp.int32) ^ group
    reducible = jnp.take(stacked, order, axis=0).astype(jnp.float32)
    ladder_out = vertex_ladder + jnp.moveaxis(reducible, 0, 1)

    crossed = []
    for channel, base in ((0, vertex_cross_a), (1, vertex_cross_b)):
        source_dev, slot_index = slots_of(tables[channel])
        slot = (source_dev * 2 + channel) * per_peer + slot_index
        row_pick = (
            slot[:, None] == jnp.arange(dev_count * 2 * per_peer, dtype=jnp.int32)[None, :]
        ).astype(jnp.bfloat16)
        column_pick = (
            jnp.arange(col_count, dtype=jnp.int32)[:, None] == col_maps[channel][None, :]
        ).astype(jnp.bfloat16)
        placed = place_rows(row_pick, column_pick, received, base.reshape(2, local_count, col_count))
        crossed.append(placed.reshape(base.shape))
    return (ladder_out, crossed[0], crossed[1])


def parts_of(q_local):
    return [tuple(range(q_local - 1, q_local // 2 - 1, -1)), tuple(range(q_local // 2 - 1, -1, -1))]


def solution(mesh):
    spread = P(None, "pb", "ka", None)

    return jax.shard_map(
        per_device,
        mesh=mesh,
        in_specs=(spread, spread, spread, P(None, "pb", None), P(), P()),
        out_specs=(spread, spread, spread),
        check_vma=False,
    )
```

profile of v0, /device:TPU:0, one launch (start us, length us, event | category | flops | bytes accessed | tf_op | source)
XLA Modules:
  0.0 172.5 jit_solution(9711274909852503714)
XLA Ops:
  0.7 1.8 %convert_element_type.61 = bf16[2,4,64,1024]{3,2,1,0:T(8,128)(2,1)S(1)} convert(f32[2,4,64,1024]{3,2,1,0:T(8,128)} %param.6) | non-fusion elementwise | flops 524288 | bytes 3145728 | tf_op jit(solution)/shard_map/convert_element_type | solution.py:193
  2.6 4.1 %collective-permute-start.9 = (bf16[2,64,1024]{2,1,0:T(8,128)(2,1)S(1)}, bf16[2,64,1024]{2,1,0:T(8,128)(2,1)S(1)}, u32[]{:S(2)}, u32[]{:S(2)}) collective-permute-start(bf16[2,64,1024]{2,1,0:T(8,128)(2,1)S(1)} %get-tuple-element.27), channel_id=1, source_target_pairs={{0,8},{1,9},{2,24},{3,25},{4,12},{5,13},{6,28},{7,29},{8,0},{9,1},... | collective-permute-start | bytes 786440 | tf_op jit(solution)/shard_map/ppermute | solution.py:191
  6.7 1.3 collective-permute-start.13
  8.1 0.7 collective-permute-start.1
  8.7 0.3 collective-permute-start.5
  9.1 3.5 %collective-permute-start = (f32[2,1024]{1,0:T(2,128)S(1)}, f32[2,1024]{1,0:T(2,128)S(1)}, u32[]{:S(2)}, u32[]{:S(2)}) collective-permute-start(f32[2,1024]{1,0:T(2,128)S(1)} %bitcast.115), channel_id=1, source_target_pairs={{0,16},{1,17},{2,18},{3,19},{4,20},{5,21},{6,22},{7,23},{8,24},{9,... | collective-permute-start | bytes 24584 | tf_op jit(solution)/shard_map/ppermute | solution.py:191
  13.3 0.1 fusion.48
  13.4 0.6 reduce-window.30
  14.0 0.1 fusion.51
  14.2 0.2 slice_reduce_fusion.2
  14.4 0.6 reduce-window.34
  15.0 0.1 fusion.15
  15.1 9.4 %collective-permute-done.9.refs_8_ = bf16[2,64,1024]{2,1,0:T(8,128)(2,1)S(1)} collective-permute-done((bf16[2,64,1024]{2,1,0:T(8,128)(2,1)S(1)}, bf16[2,64,1024]{2,1,0:T(8,128)(2,1)S(1)}, u32[]{:S(2)}, u32[]{:S(2)}) %collective-permute-start.9) | collective-permute-done | bytes 262176 | tf_op jit(solution)/shard_map/ppermute | solution.py:191
  24.5 2.1 %collective-permute-start.11 = (bf16[2,64,1024]{2,1,0:T(8,128)(2,1)S(1)}, bf16[2,64,1024]{2,1,0:T(8,128)(2,1)S(1)}, u32[]{:S(2)}, u32[]{:S(2)}) collective-permute-start(bf16[2,64,1024]{2,1,0:T(8,128)(2,1)S(1)} %collective-permute-done.9.refs_8_), channel_id=1, source_target_pairs={{0,1},{1,0},{2,3},{3,2},{4,5},{5,4},{6,7},{7,6},{8,9},{9,8},{10,11... | collective-permute-start | bytes 786440 | tf_op jit(solution)/shard_map/ppermute | solution.py:191
  26.8 0.2 slice_reduce_fusion.1
  27.0 0.7 collective-permute-start.10
  27.9 1.7 collective-permute-start.3
  29.6 3.9 %collective-permute-done.11.refs_10_ = bf16[2,64,1024]{2,1,0:T(8,128)(2,1)S(1)} collective-permute-done((bf16[2,64,1024]{2,1,0:T(8,128)(2,1)S(1)}, bf16[2,64,1024]{2,1,0:T(8,128)(2,1)S(1)}, u32[]{:S(2)}, u32[]{:S(2)}) %collective-permute-start.11) | collective-permute-done | bytes 262176 | tf_op jit(solution)/shard_map/ppermute | solution.py:191
  33.5 0.8 collective-permute-start.2
  34.3 4.8 %collective-permute-done.15.refs_14_ = bf16[2,64,1024]{2,1,0:T(8,128)(2,1)S(1)} collective-permute-done((bf16[2,64,1024]{2,1,0:T(8,128)(2,1)S(1)}, bf16[2,64,1024]{2,1,0:T(8,128)(2,1)S(1)}, u32[]{:S(2)}, u32[]{:S(2)}) %collective-permute-start.15) | collective-permute-done | bytes 262176 | tf_op jit(solution)/shard_map/ppermute | solution.py:191
  39.1 2.4 %collective-permute-start.7 = (bf16[2,64,1024]{2,1,0:T(8,128)(2,1)S(1)}, bf16[2,64,1024]{2,1,0:T(8,128)(2,1)S(1)}, u32[]{:S(2)}, u32[]{:S(2)}) collective-permute-start(bf16[2,64,1024]{2,1,0:T(8,128)(2,1)S(1)} %collective-permute-done.5.refs_4_), channel_id=1, source_target_pairs={{0,1},{1,0},{2,3},{3,2},{4,5},{5,4},{6,7},{7,6},{8,9},{9,8},{10,11... | collective-permute-start | bytes 786440 | tf_op jit(solution)/shard_map/ppermute | solution.py:191
  41.5 0.6 multiply_reduce_fusion.1
  42.2 0.6 multiply_reduce_fusion
  42.8 1.9 %collective-permute-done.3.refs_2_ = bf16[2,64,1024]{2,1,0:T(8,128)(2,1)S(1)} collective-permute-done((bf16[2,64,1024]{2,1,0:T(8,128)(2,1)S(1)}, bf16[2,64,1024]{2,1,0:T(8,128)(2,1)S(1)}, u32[]{:S(2)}, u32[]{:S(2)}) %collective-permute-start.3) | collective-permute-done | bytes 262176 | tf_op jit(solution)/shard_map/ppermute | solution.py:191
  44.7 0.8 collective-permute-start.6
  45.5 4.8 %collective-permute-done.7.refs_6_ = bf16[2,64,1024]{2,1,0:T(8,128)(2,1)S(1)} collective-permute-done((bf16[2,64,1024]{2,1,0:T(8,128)(2,1)S(1)}, bf16[2,64,1024]{2,1,0:T(8,128)(2,1)S(1)}, u32[]{:S(2)}, u32[]{:S(2)}) %collective-permute-start.7) | collective-permute-done | bytes 262176 | tf_op jit(solution)/shard_map/ppermute | solution.py:191
  50.3 0.2 collective-permute-start.12
  50.5 0.4 collective-permute-start.16
  50.9 0.2 collective-permute-start.4
  51.0 0.4 collective-permute-start.8
  51.4 0.7 pad_add_fusion.1.place_ref
  52.0 0.6 broadcast_select_fusion.chi_ref
  52.8 0.4 collective-permute-done.8.refs_7_
  53.2 0.1 copy-done.22
  53.3 10.8 %ladder.2 = (bf16[2,64,1024]{2,1,0:T(8,128)(2,1)}, bf16[2,64,1024]{2,1,0:T(8,128)(2,1)}) custom-call(s32[3]{0:T(128)} %pad_add_fusion.1.place_ref, f32[2,1024]{1,0:T(2,128)} %broadcast_select_fusion.chi_ref, bf16[2,64,1024]{2,1,0:T(8,128)(2,1)} %copy-done.13, bf16[2,64,1024]{2,1,0:T(8,128)(2,1)} %copy-done.20, bf16[2,64,1024]{2,1,0:T(8,128)(2,1)} %copy-done.19, ...), custom_call_target="tpu_custom_call" | custom-call | flops 6442450944 | bytes 5242880 | tf_op jit(solution)/shard_map/ladder/pallas_call | solution.py:87
  64.2 1.1 collective-permute-start.18
  65.3 11.1 %ladder.3 = (bf16[2,64,1024]{2,1,0:T(8,128)(2,1)}, bf16[2,64,1024]{2,1,0:T(8,128)(2,1)}) custom-call(s32[3]{0:T(128)} %pad_add_fusion.1.place_ref, f32[2,1024]{1,0:T(2,128)} %broadcast_select_fusion.chi_ref, bf16[2,64,1024]{2,1,0:T(8,128)(2,1)} %copy-done.13, bf16[2,64,1024]{2,1,0:T(8,128)(2,1)} %copy-done.20, bf16[2,64,1024]{2,1,0:T(8,128)(2,1)} %copy-done.19, ...), custom_call_target="tpu_custom_call" | custom-call | flops 6442450944 | bytes 5242880 | tf_op jit(solution)/shard_map/ladder/pallas_call | solution.py:87
  76.4 3.0 %collective-permute-start.20 = (bf16[2,64,1024]{2,1,0:T(8,128)(2,1)}, bf16[2,64,1024]{2,1,0:T(8,128)(2,1)S(1)}, u32[]{:S(2)}, u32[]{:S(2)}) collective-permute-start(bf16[2,64,1024]{2,1,0:T(8,128)(2,1)} %get-tuple-element.9), channel_id=1, source_target_pairs={{0,8},{1,9},{2,10},{3,11},{4,12},{5,13},{6,14},{7,15},{8,0},{9,1},... | collective-permute-start | bytes 786440 | tf_op jit(solution)/shard_map/ppermute | solution.py:191
  79.4 0.4 collective-permute-start.22
  79.9 0.8 fusion.3.chosen_ref
  80.8 16.6 %collective-permute-done.20.refs_2_ = bf16[2,64,1024]{2,1,0:T(8,128)(2,1)S(1)} collective-permute-done((bf16[2,64,1024]{2,1,0:T(8,128)(2,1)}, bf16[2,64,1024]{2,1,0:T(8,128)(2,1)S(1)}, u32[]{:S(2)}, u32[]{:S(2)}) %collective-permute-start.20) | collective-permute-done | bytes 262176 | tf_op jit(solution)/shard_map/ppermute | solution.py:191
  97.4 0.7 copy-done.5
  98.2 3.3 %select_rows.1 = bf16[512,2048]{1,0:T(8,128)(2,1)} custom-call(bf16[512,256]{1,0:T(8,128)(2,1)} %fusion.3.chosen_ref, bf16[2,64,1024]{2,1,0:T(8,128)(2,1)} %get-tuple-element.7.refs_0_, bf16[2,64,1024]{2,1,0:T(8,128)(2,1)} %copy-done.3, bf16[2,64,1024]{2,1,0:T(8,128)(2,1)} %copy-done.5, bf16[2,64,1024]{2,1,0:T(8,128)(2,1)} %copy-done.7), custom_call_target="tpu_custom_call" | custom-call | flops 536870912 | bytes 4194304 | tf_op jit(solution)/shard_map/select_rows/pallas_call | solution.py:124
  101.5 8.5 %all-to-all-start = ((bf16[32,16,2048]{2,1,0:T(8,128)(2,1)}), bf16[32,16,2048]{2,1,0:T(8,128)(2,1)S(1)}, u32[]{:S(2)}, u32[]{:S(2)}) async-start(bf16[32,16,2048]{2,1,0:T(8,128)(2,1)} %bitcast.94), calls=%async_computation | async-start | bytes 4194304 | tf_op jit(solution)/shard_map/all_to_all | solution.py:258
  110.1 0.6 reduce-window.36
  110.7 0.2 slice_reduce_fusion
  110.9 0.6 reduce-window.26
  111.5 0.2 slice_reduce_fusion.3
  112.1 0.8 fusion.4.rows_ref
  112.9 0.8 fusion.2.rows_ref
  113.7 2.2 %fusion.1.columns_ref = bf16[1024,1024]{1,0:T(8,128)(2,1)} fusion(s32[1024]{0:T(1024)S(1)} %bitcast.110), kind=kLoop, calls=%fused_computation.4 | loop fusion | flops 2097152 | bytes 2101248 | tf_op jit(solution)/shard_map/convert_element_type | solution.py:276
  115.9 0.7 collective-permute-start.17
  116.6 0.7 collective-permute-start.19
  117.3 0.7 collective-permute-start.23
  118.0 0.7 collective-permute-start.21
  118.7 2.2 %fusion.columns_ref = bf16[1024,1024]{1,0:T(8,128)(2,1)} fusion(s32[1024]{0:T(1024)S(1)} %bitcast.109), kind=kLoop, calls=%fused_computation.3 | loop fusion | flops 2097152 | bytes 2101248 | tf_op jit(solution)/shard_map/convert_element_type | solution.py:276
  120.9 0.1 pad_maximum_fusion
  121.1 1.6 gather_fusion
  122.7 2.2 %bitcast_add_fusion = f32[2,4,64,1024]{3,2,0,1:T(8,128)S(1)} fusion(f32[2,4,64,1024]{3,2,1,0:T(8,128)} %param.6, bf16[4,2,64,1024]{3,2,1,0:T(8,128)(2,1)} %gather_fusion, pred[4]{0:T(512)(128)(4,1)S(1)} %compare_and_fusion), kind=kLoop, calls=%fused_computation.5 | loop fusion | flops 1572864 | bytes 5242884 | tf_op jit(solution)/shard_map/add | solution.py:265
  124.9 1.5 copy.79
  126.4 34.2 %all-to-all-done = bf16[32,16,2048]{2,1,0:T(8,128)(2,1)S(1)} async-done(((bf16[32,16,2048]{2,1,0:T(8,128)(2,1)}), bf16[32,16,2048]{2,1,0:T(8,128)(2,1)S(1)}, u32[]{:S(2)}, u32[]{:S(2)}) %all-to-all-start) | async-done | bytes 2097184 | tf_op jit(solution)/shard_map/all_to_all | solution.py:258
  160.6 1.3 copy-done.1
  161.9 5.3 %place_rows.3 = f32[2,256,1024]{2,1,0:T(8,128)} custom-call(bf16[256,512]{1,0:T(8,128)(2,1)} %fusion.4.rows_ref, bf16[1024,1024]{1,0:T(8,128)(2,1)} %fusion.1.columns_ref, bf16[512,2048]{1,0:T(8,128)(2,1)} %bitcast.92, f32[2,256,1024]{2,1,0:T(8,128)} %bitcast.95), custom_call_target="tpu_custom_call" | custom-call | flops 1610612736 | bytes 6291456 | tf_op jit(solution)/shard_map/place_rows/pallas_call | solution.py:148
  167.2 5.3 %place_rows.2 = f32[2,256,1024]{2,1,0:T(8,128)} custom-call(bf16[256,512]{1,0:T(8,128)(2,1)} %fusion.2.rows_ref, bf16[1024,1024]{1,0:T(8,128)(2,1)} %fusion.columns_ref, bf16[512,2048]{1,0:T(8,128)(2,1)} %bitcast.93, f32[2,256,1024]{2,1,0:T(8,128)} %bitcast.96), custom_call_target="tpu_custom_call" | custom-call | flops 1610612736 | bytes 6291456 | tf_op jit(solution)/shard_map/place_rows/pallas_call | solution.py:148
  (101 shorter events, 2.0 us)
Async XLA Ops:
  0.6 8.4 %copy-start = (f32[2,4,1024]{2,1,0:T(4,128)S(1)}, f32[2,4,1024]{2,1,0:T(4,128)}, u32[]{:S(2)}) copy-start(f32[2,4,1024]{2,1,0:T(4,128)} %param.9) | copy-start | bytes 98308
  0.7 11.9 %copy-start.9 = (s32[2,8,1024]{2,1,0:T(8,128)S(1)}, s32[2,8,1024]{2,1,0:T(8,128)}, u32[]{:S(2)}) copy-start(s32[2,8,1024]{2,1,0:T(8,128)} %param.10) | copy-start | bytes 196612
  2.6 21.9 %collective-permute-start.9 = (bf16[2,64,1024]{2,1,0:T(8,128)(2,1)S(1)}, bf16[2,64,1024]{2,1,0:T(8,128)(2,1)S(1)}, u32[]{:S(2)}, u32[]{:S(2)}) collective-permute-start(bf16[2,64,1024]{2,1,0:T(8,128)(2,1)S(1)} %get-tuple-element.27), channel_id=1, source_target_pairs={{0,8},{1,9},{2,24},{3,25},{4,12},{5,13},{6,28},{7,29},{8,0},{9,1},... | collective-permute-start | bytes 786440 | tf_op jit(solution)/shard_map/ppermute | solution.py:191
  6.7 19.9 %collective-permute-start.13 = (bf16[2,64,1024]{2,1,0:T(8,128)(2,1)S(1)}, bf16[2,64,1024]{2,1,0:T(8,128)(2,1)S(1)}, u32[]{:S(2)}, u32[]{:S(2)}) collective-permute-start(bf16[2,64,1024]{2,1,0:T(8,128)(2,1)S(1)} %get-tuple-element.26), channel_id=1, source_target_pairs={{0,12},{1,13},{2,28},{3,29},{4,8},{5,9},{6,24},{7,25},{8,4},{9,5},... | collective-permute-start | bytes 786440 | tf_op jit(solution)/shard_map/ppermute | solution.py:191
  8.1 19.7 %collective-permute-start.1 = (bf16[2,64,1024]{2,1,0:T(8,128)(2,1)S(1)}, bf16[2,64,1024]{2,1,0:T(8,128)(2,1)S(1)}, u32[]{:S(2)}, u32[]{:S(2)}) collective-permute-start(bf16[2,64,1024]{2,1,0:T(8,128)(2,1)S(1)} %get-tuple-element.29), channel_id=1, source_target_pairs={{0,0},{1,1},{2,16},{3,17},{4,4},{5,5},{6,20},{7,21},{8,8},{9,9},{1... | collective-permute-start | bytes 786440 | tf_op jit(solution)/shard_map/ppermute | solution.py:191
  8.7 19.1 %collective-permute-start.5 = (bf16[2,64,1024]{2,1,0:T(8,128)(2,1)S(1)}, bf16[2,64,1024]{2,1,0:T(8,128)(2,1)S(1)}, u32[]{:S(2)}, u32[]{:S(2)}) collective-permute-start(bf16[2,64,1024]{2,1,0:T(8,128)(2,1)S(1)} %get-tuple-element.28), channel_id=1, source_target_pairs={{0,4},{1,5},{2,20},{3,21},{4,0},{5,1},{6,16},{7,17},{8,12},{9,13},... | collective-permute-start | bytes 786440 | tf_op jit(solution)/shard_map/ppermute | solution.py:191
  9.1 18.0 %collective-permute-start = (f32[2,1024]{1,0:T(2,128)S(1)}, f32[2,1024]{1,0:T(2,128)S(1)}, u32[]{:S(2)}, u32[]{:S(2)}) collective-permute-start(f32[2,1024]{1,0:T(2,128)S(1)} %bitcast.115), channel_id=1, source_target_pairs={{0,16},{1,17},{2,18},{3,19},{4,20},{5,21},{6,22},{7,23},{8,24},{9,... | collective-permute-start | bytes 24584 | tf_op jit(solution)/shard_map/ppermute | solution.py:191
  24.5 28.6 %copy-start.11 = (bf16[2,64,1024]{2,1,0:T(8,128)(2,1)}, bf16[2,64,1024]{2,1,0:T(8,128)(2,1)S(1)}, u32[]{:S(2)}) copy-start(bf16[2,64,1024]{2,1,0:T(8,128)(2,1)S(1)} %collective-permute-done.9.refs_8_) | copy-start | bytes 786436
  24.5 9.0 %collective-permute-start.11 = (bf16[2,64,1024]{2,1,0:T(8,128)(2,1)S(1)}, bf16[2,64,1024]{2,1,0:T(8,128)(2,1)S(1)}, u32[]{:S(2)}, u32[]{:S(2)}) collective-permute-start(bf16[2,64,1024]{2,1,0:T(8,128)(2,1)S(1)} %collective-permute-done.9.refs_8_), channel_id=1, source_target_pairs={{0,1},{1,0},{2,3},{3,2},{4,5},{5,4},{6,7},{7,6},{8,9},{9,8},{10,11... | collective-permute-start | bytes 786440 | tf_op jit(solution)/shard_map/ppermute | solution.py:191
  26.7 26.5 %copy-start.12 = (bf16[2,64,1024]{2,1,0:T(8,128)(2,1)}, bf16[2,64,1024]{2,1,0:T(8,128)(2,1)S(1)}, u32[]{:S(2)}) copy-start(bf16[2,64,1024]{2,1,0:T(8,128)(2,1)S(1)} %collective-permute-done.13.refs_12_) | copy-start | bytes 786436
  26.7 12.4 %collective-permute-start.15 = (bf16[2,64,1024]{2,1,0:T(8,128)(2,1)S(1)}, bf16[2,64,1024]{2,1,0:T(8,128)(2,1)S(1)}, u32[]{:S(2)}, u32[]{:S(2)}) collective-permute-start(bf16[2,64,1024]{2,1,0:T(8,128)(2,1)S(1)} %collective-permute-done.13.refs_12_), channel_id=1, source_target_pairs={{0,1},{1,0},{2,3},{3,2},{4,5},{5,4},{6,7},{7,6},{8,9},{9,8},{10,11... | collective-permute-start | bytes 786440 | tf_op jit(solution)/shard_map/ppermute | solution.py:191
  27.0 23.5 %collective-permute-start.10 = (bf16[2,64,1024]{2,1,0:T(8,128)(2,1)S(1)}, bf16[2,64,1024]{2,1,0:T(8,128)(2,1)S(1)}, u32[]{:S(2)}, u32[]{:S(2)}) collective-permute-start(bf16[2,64,1024]{2,1,0:T(8,128)(2,1)S(1)} %collective-permute-done.9.refs_8_), channel_id=1, source_target_pairs={{0,16},{1,17},{2,18},{3,19},{4,20},{5,21},{6,22},{7,23},{8,24},{9,... | collective-permute-start | bytes 786440 | tf_op jit(solution)/shard_map/ppermute | solution.py:191
  27.8 25.4 %copy-start.13 = (bf16[2,64,1024]{2,1,0:T(8,128)(2,1)}, bf16[2,64,1024]{2,1,0:T(8,128)(2,1)S(1)}, u32[]{:S(2)}) copy-start(bf16[2,64,1024]{2,1,0:T(8,128)(2,1)S(1)} %collective-permute-done.1.refs_0_) | copy-start | bytes 786436
  27.8 23.1 %collective-permute-start.14 = (bf16[2,64,1024]{2,1,0:T(8,128)(2,1)S(1)}, bf16[2,64,1024]{2,1,0:T(8,128)(2,1)S(1)}, u32[]{:S(2)}, u32[]{:S(2)}) collective-permute-start(bf16[2,64,1024]{2,1,0:T(8,128)(2,1)S(1)} %collective-permute-done.13.refs_12_), channel_id=1, source_target_pairs={{0,16},{1,17},{2,18},{3,19},{4,20},{5,21},{6,22},{7,23},{8,24},{9,... | collective-permute-start | bytes 786440 | tf_op jit(solution)/shard_map/ppermute | solution.py:191
  27.9 25.3 %copy-start.14 = (bf16[2,64,1024]{2,1,0:T(8,128)(2,1)}, bf16[2,64,1024]{2,1,0:T(8,128)(2,1)S(1)}, u32[]{:S(2)}) copy-start(bf16[2,64,1024]{2,1,0:T(8,128)(2,1)S(1)} %collective-permute-done.5.refs_4_) | copy-start | bytes 786436
  27.9 16.8 %collective-permute-start.3 = (bf16[2,64,1024]{2,1,0:T(8,128)(2,1)S(1)}, bf16[2,64,1024]{2,1,0:T(8,128)(2,1)S(1)}, u32[]{:S(2)}, u32[]{:S(2)}) collective-permute-start(bf16[2,64,1024]{2,1,0:T(8,128)(2,1)S(1)} %collective-permute-done.1.refs_0_), channel_id=1, source_target_pairs={{0,1},{1,0},{2,3},{3,2},{4,5},{5,4},{6,7},{7,6},{8,9},{9,8},{10,11... | collective-permute-start | bytes 786440 | tf_op jit(solution)/shard_map/ppermute | solution.py:191
  33.5 19.7 %copy-start.15 = (bf16[2,64,1024]{2,1,0:T(8,128)(2,1)}, bf16[2,64,1024]{2,1,0:T(8,128)(2,1)S(1)}, u32[]{:S(2)}) copy-start(bf16[2,64,1024]{2,1,0:T(8,128)(2,1)S(1)} %collective-permute-done.11.refs_10_) | copy-start | bytes 786436
  33.5 17.5 %collective-permute-start.2 = (bf16[2,64,1024]{2,1,0:T(8,128)(2,1)S(1)}, bf16[2,64,1024]{2,1,0:T(8,128)(2,1)S(1)}, u32[]{:S(2)}, u32[]{:S(2)}) collective-permute-start(bf16[2,64,1024]{2,1,0:T(8,128)(2,1)S(1)} %collective-permute-done.1.refs_0_), channel_id=1, source_target_pairs={{0,16},{1,17},{2,18},{3,19},{4,20},{5,21},{6,22},{7,23},{8,24},{9,... | collective-permute-start | bytes 786440 | tf_op jit(solution)/shard_map/ppermute | solution.py:191
  39.1 14.1 %copy-start.16 = (bf16[2,64,1024]{2,1,0:T(8,128)(2,1)}, bf16[2,64,1024]{2,1,0:T(8,128)(2,1)S(1)}, u32[]{:S(2)}) copy-start(bf16[2,64,1024]{2,1,0:T(8,128)(2,1)S(1)} %collective-permute-done.15.refs_14_) | copy-start | bytes 786436
  39.1 11.2 %collective-permute-start.7 = (bf16[2,64,1024]{2,1,0:T(8,128)(2,1)S(1)}, bf16[2,64,1024]{2,1,0:T(8,128)(2,1)S(1)}, u32[]{:S(2)}, u32[]{:S(2)}) collective-permute-start(bf16[2,64,1024]{2,1,0:T(8,128)(2,1)S(1)} %collective-permute-done.5.refs_4_), channel_id=1, source_target_pairs={{0,1},{1,0},{2,3},{3,2},{4,5},{5,4},{6,7},{7,6},{8,9},{9,8},{10,11... | collective-permute-start | bytes 786440 | tf_op jit(solution)/shard_map/ppermute | solution.py:191
  44.7 8.5 %copy-start.19 = (bf16[2,64,1024]{2,1,0:T(8,128)(2,1)}, bf16[2,64,1024]{2,1,0:T(8,128)(2,1)S(1)}, u32[]{:S(2)}) copy-start(bf16[2,64,1024]{2,1,0:T(8,128)(2,1)S(1)} %collective-permute-done.3.refs_2_) | copy-start | bytes 786436
  44.7 7.9 %collective-permute-start.6 = (bf16[2,64,1024]{2,1,0:T(8,128)(2,1)S(1)}, bf16[2,64,1024]{2,1,0:T(8,128)(2,1)S(1)}, u32[]{:S(2)}, u32[]{:S(2)}) collective-permute-start(bf16[2,64,1024]{2,1,0:T(8,128)(2,1)S(1)} %collective-permute-done.5.refs_4_), channel_id=1, source_target_pairs={{0,16},{1,17},{2,18},{3,19},{4,20},{5,21},{6,22},{7,23},{8,24},{9,... | collective-permute-start | bytes 786440 | tf_op jit(solution)/shard_map/ppermute | solution.py:191
  50.3 2.8 %copy-start.21 = (bf16[2,64,1024]{2,1,0:T(8,128)(2,1)}, bf16[2,64,1024]{2,1,0:T(8,128)(2,1)S(1)}, u32[]{:S(2)}) copy-start(bf16[2,64,1024]{2,1,0:T(8,128)(2,1)S(1)} %collective-permute-done.7.refs_6_) | copy-start | bytes 786436
  50.3 2.3 %collective-permute-start.12 = (bf16[2,64,1024]{2,1,0:T(8,128)(2,1)S(1)}, bf16[2,64,1024]{2,1,0:T(8,128)(2,1)}, u32[]{:S(2)}, u32[]{:S(2)}) collective-permute-start(bf16[2,64,1024]{2,1,0:T(8,128)(2,1)S(1)} %collective-permute-done.11.refs_10_), channel_id=1, source_target_pairs={{0,16},{1,17},{2,18},{3,19},{4,20},{5,21},{6,22},{7,23},{8,24},{9,... | collective-permute-start | bytes 786440 | tf_op jit(solution)/shard_map/ppermute | solution.py:191
  50.5 2.7 %copy-start.17 = (bf16[2,64,1024]{2,1,0:T(8,128)(2,1)}, bf16[2,64,1024]{2,1,0:T(8,128)(2,1)S(1)}, u32[]{:S(2)}) copy-start(bf16[2,64,1024]{2,1,0:T(8,128)(2,1)S(1)} %collective-permute-done.10.refs_9_) | copy-start | bytes 786436
  50.5 2.1 %collective-permute-start.16 = (bf16[2,64,1024]{2,1,0:T(8,128)(2,1)S(1)}, bf16[2,64,1024]{2,1,0:T(8,128)(2,1)}, u32[]{:S(2)}, u32[]{:S(2)}) collective-permute-start(bf16[2,64,1024]{2,1,0:T(8,128)(2,1)S(1)} %collective-permute-done.15.refs_14_), channel_id=1, source_target_pairs={{0,16},{1,17},{2,18},{3,19},{4,20},{5,21},{6,22},{7,23},{8,24},{9,... | collective-permute-start | bytes 786440 | tf_op jit(solution)/shard_map/ppermute | solution.py:191
  50.9 2.3 %copy-start.18 = (bf16[2,64,1024]{2,1,0:T(8,128)(2,1)}, bf16[2,64,1024]{2,1,0:T(8,128)(2,1)S(1)}, u32[]{:S(2)}) copy-start(bf16[2,64,1024]{2,1,0:T(8,128)(2,1)S(1)} %collective-permute-done.14.refs_13_) | copy-start | bytes 786436
  50.9 1.9 %collective-permute-start.4 = (bf16[2,64,1024]{2,1,0:T(8,128)(2,1)S(1)}, bf16[2,64,1024]{2,1,0:T(8,128)(2,1)}, u32[]{:S(2)}, u32[]{:S(2)}) collective-permute-start(bf16[2,64,1024]{2,1,0:T(8,128)(2,1)S(1)} %collective-permute-done.3.refs_2_), channel_id=1, source_target_pairs={{0,16},{1,17},{2,18},{3,19},{4,20},{5,21},{6,22},{7,23},{8,24},{9,... | collective-permute-start | bytes 786440 | tf_op jit(solution)/shard_map/ppermute | solution.py:191
  51.0 2.2 %copy-start.20 = (bf16[2,64,1024]{2,1,0:T(8,128)(2,1)}, bf16[2,64,1024]{2,1,0:T(8,128)(2,1)S(1)}, u32[]{:S(2)}) copy-start(bf16[2,64,1024]{2,1,0:T(8,128)(2,1)S(1)} %collective-permute-done.2.refs_1_) | copy-start | bytes 786436
  51.0 2.1 %collective-permute-start.8 = (bf16[2,64,1024]{2,1,0:T(8,128)(2,1)S(1)}, bf16[2,64,1024]{2,1,0:T(8,128)(2,1)}, u32[]{:S(2)}, u32[]{:S(2)}) collective-permute-start(bf16[2,64,1024]{2,1,0:T(8,128)(2,1)S(1)} %collective-permute-done.7.refs_6_), channel_id=1, source_target_pairs={{0,16},{1,17},{2,18},{3,19},{4,20},{5,21},{6,22},{7,23},{8,24},{9,... | collective-permute-start | bytes 786440 | tf_op jit(solution)/shard_map/ppermute | solution.py:191
  52.6 0.7 copy-start.22
  64.2 16.6 %collective-permute-start.18 = (bf16[2,64,1024]{2,1,0:T(8,128)(2,1)}, bf16[2,64,1024]{2,1,0:T(8,128)(2,1)S(1)}, u32[]{:S(2)}, u32[]{:S(2)}) collective-permute-start(bf16[2,64,1024]{2,1,0:T(8,128)(2,1)} %get-tuple-element.8), channel_id=1, source_target_pairs={{0,4},{1,5},{2,6},{3,7},{4,0},{5,1},{6,2},{7,3},{8,12},{9,13},{10,... | collective-permute-start | bytes 786440 | tf_op jit(solution)/shard_map/ppermute | solution.py:191
  76.4 21.0 %collective-permute-start.20 = (bf16[2,64,1024]{2,1,0:T(8,128)(2,1)}, bf16[2,64,1024]{2,1,0:T(8,128)(2,1)S(1)}, u32[]{:S(2)}, u32[]{:S(2)}) collective-permute-start(bf16[2,64,1024]{2,1,0:T(8,128)(2,1)} %get-tuple-element.9), channel_id=1, source_target_pairs={{0,8},{1,9},{2,10},{3,11},{4,12},{5,13},{6,14},{7,15},{8,0},{9,1},... | collective-permute-start | bytes 786440 | tf_op jit(solution)/shard_map/ppermute | solution.py:191
  79.4 18.0 %collective-permute-start.22 = (bf16[2,64,1024]{2,1,0:T(8,128)(2,1)}, bf16[2,64,1024]{2,1,0:T(8,128)(2,1)S(1)}, u32[]{:S(2)}, u32[]{:S(2)}) collective-permute-start(bf16[2,64,1024]{2,1,0:T(8,128)(2,1)} %get-tuple-element.10), channel_id=1, source_target_pairs={{0,12},{1,13},{2,14},{3,15},{4,8},{5,9},{6,10},{7,11},{8,4},{9,5},... | collective-permute-start | bytes 786440 | tf_op jit(solution)/shard_map/ppermute | solution.py:191
  80.8 16.6 %copy-start.3 = (bf16[2,64,1024]{2,1,0:T(8,128)(2,1)}, bf16[2,64,1024]{2,1,0:T(8,128)(2,1)S(1)}, u32[]{:S(2)}) copy-start(bf16[2,64,1024]{2,1,0:T(8,128)(2,1)S(1)} %collective-permute-done.18.refs_1_) | copy-start | bytes 786436
  97.4 0.7 copy-start.5
  97.4 0.8 copy-start.7
  101.5 10.6 %copy-start.10 = (s32[2,1024]{1,0:T(2,128)S(1)}, s32[2,1024]{1,0:T(2,128)}, u32[]{:S(2)}) copy-start(s32[2,1024]{1,0:T(2,128)} %param.11) | copy-start | bytes 24580
  101.5 59.1 %all-to-all-start = ((bf16[32,16,2048]{2,1,0:T(8,128)(2,1)}), bf16[32,16,2048]{2,1,0:T(8,128)(2,1)S(1)}, u32[]{:S(2)}, u32[]{:S(2)}) async-start(bf16[32,16,2048]{2,1,0:T(8,128)(2,1)} %bitcast.94), calls=%async_computation | async-start | bytes 4194304 | tf_op jit(solution)/shard_map/all_to_all | solution.py:258
  110.0 6.0 %copy-start.2 = (bf16[2,64,1024]{2,1,0:T(8,128)(2,1)S(1)}, bf16[2,64,1024]{2,1,0:T(8,128)(2,1)}, u32[]{:S(2)}) copy-start(bf16[2,64,1024]{2,1,0:T(8,128)(2,1)} %get-tuple-element.7.refs_0_) | copy-start | bytes 786436
  110.0 6.6 %copy-start.4 = (bf16[2,64,1024]{2,1,0:T(8,128)(2,1)S(1)}, bf16[2,64,1024]{2,1,0:T(8,128)(2,1)}, u32[]{:S(2)}) copy-start(bf16[2,64,1024]{2,1,0:T(8,128)(2,1)} %copy-done.3) | copy-start | bytes 786436
  110.0 7.3 %copy-start.8 = (bf16[2,64,1024]{2,1,0:T(8,128)(2,1)S(1)}, bf16[2,64,1024]{2,1,0:T(8,128)(2,1)}, u32[]{:S(2)}) copy-start(bf16[2,64,1024]{2,1,0:T(8,128)(2,1)} %copy-done.7) | copy-start | bytes 786436
  110.0 8.0 %copy-start.6 = (bf16[2,64,1024]{2,1,0:T(8,128)(2,1)S(1)}, bf16[2,64,1024]{2,1,0:T(8,128)(2,1)}, u32[]{:S(2)}) copy-start(bf16[2,64,1024]{2,1,0:T(8,128)(2,1)} %copy-done.5) | copy-start | bytes 786436
  115.9 5.0 %collective-permute-start.17 = (bf16[2,64,1024]{2,1,0:T(8,128)(2,1)S(1)}, bf16[2,64,1024]{2,1,0:T(8,128)(2,1)S(1)}, u32[]{:S(2)}, u32[]{:S(2)}) collective-permute-start(bf16[2,64,1024]{2,1,0:T(8,128)(2,1)S(1)} %copy-done.2), channel_id=1, source_target_pairs={{0,0},{1,1},{2,16},{3,17},{4,4},{5,5},{6,20},{7,21},{8,8},{9,9},{1... | collective-permute-start | bytes 786440 | tf_op jit(solution)/shard_map/ppermute | solution.py:191
  116.6 4.3 %collective-permute-start.19 = (bf16[2,64,1024]{2,1,0:T(8,128)(2,1)S(1)}, bf16[2,64,1024]{2,1,0:T(8,128)(2,1)S(1)}, u32[]{:S(2)}, u32[]{:S(2)}) collective-permute-start(bf16[2,64,1024]{2,1,0:T(8,128)(2,1)S(1)} %copy-done.4), channel_id=1, source_target_pairs={{0,0},{1,1},{2,16},{3,17},{4,4},{5,5},{6,20},{7,21},{8,8},{9,9},{1... | collective-permute-start | bytes 786440 | tf_op jit(solution)/shard_map/ppermute | solution.py:191
  117.3 3.6 %collective-permute-start.23 = (bf16[2,64,1024]{2,1,0:T(8,128)(2,1)S(1)}, bf16[2,64,1024]{2,1,0:T(8,128)(2,1)S(1)}, u32[]{:S(2)}, u32[]{:S(2)}) collective-permute-start(bf16[2,64,1024]{2,1,0:T(8,128)(2,1)S(1)} %copy-done.8), channel_id=1, source_target_pairs={{0,0},{1,1},{2,16},{3,17},{4,4},{5,5},{6,20},{7,21},{8,8},{9,9},{1... | collective-permute-start | bytes 786440 | tf_op jit(solution)/shard_map/ppermute | solution.py:191
  118.0 2.9 %collective-permute-start.21 = (bf16[2,64,1024]{2,1,0:T(8,128)(2,1)S(1)}, bf16[2,64,1024]{2,1,0:T(8,128)(2,1)S(1)}, u32[]{:S(2)}, u32[]{:S(2)}) collective-permute-start(bf16[2,64,1024]{2,1,0:T(8,128)(2,1)S(1)} %copy-done.6), channel_id=1, source_target_pairs={{0,0},{1,1},{2,16},{3,17},{4,4},{5,5},{6,20},{7,21},{8,8},{9,9},{1... | collective-permute-start | bytes 786440 | tf_op jit(solution)/shard_map/ppermute | solution.py:191
  160.6 1.3 copy-start.1
where the time goes:
time: 173 us; the launch traced here: 172 us
  waiting for transfers between devices  76.3 us (44%)
  Pallas kernels  35.8 us (21%)
  starting transfers between devices  35.3 us (20%)
  other arithmetic  16.9 us (10%)
  local copies, waits for them, and re-layouts  6.98 us (4%)
    ppermute x24, waiting for transfers between devices, move(): lax.ppermute(value, ('pb', 'ka'), [(i, target(i)) for i in range(dev_coun...  42.1 us
    all_to_all x1, waiting for transfers between devices, per_device(): lax.all_to_all(send.reshape(dev_count, 2 * per_peer, 2 * col_count), ('pb...  34.2 us
    ppermute x24, starting transfers between devices, move(): lax.ppermute(value, ('pb', 'ka'), [(i, target(i)) for i in range(dev_coun...  26.9 us
    pallas_call x2, Pallas kernels, ladder(): pl.pallas_call(functools.partial(ladder_kernel, groups, low_count, wanted...  21.9 us
    pallas_call x2, Pallas kernels, place_rows(): pl.pallas_call(place_kernel, out_shape=jax.ShapeDtypeStruct((2, count, de...  10.6 us
    all_to_all x1, starting transfers between devices, per_device(): lax.all_to_all(send.reshape(dev_count, 2 * per_peer, 2 * col_count), ('pb...  8.45 us
    convert_element_type x2, other arithmetic, per_device(): column_pick = (jnp.arange(col_count, dtype=jnp.int32)[:, None] == col_map...  4.42 us
    unnamed x48, local copies, waits for them, and re-layouts  3.77 us
  transfers between devices with their start and end apart: 25, of which 9 were waited for; matrix products, arithmetic and copies ran while one was open for 11% of the time, Pallas kernels for 6%

commit v1 on v0

--- a/solution.py
+++ b/solution.py
@@ -10,6 +10,8 @@
 
 LADDER = 6
 TILE = 256
+MIB = 1 << 20
+SELECT_VMEM = 14 * MIB
 
 
 def ladder_kernel(groups, low_count, wanted, place_ref, chi_ref, *refs):
@@ -129,40 +131,52 @@
             bytes_accessed=8 * chosen.shape[0] * depth,
             transcendentals=0,
         ),
+        compiler_params=pltpu.CompilerParams(vmem_limit_bytes=SELECT_VMEM),
         name="select_rows",
     )(chosen, *returned)
 
 
-def place_kernel(rows_ref, columns_ref, received_ref, base_ref, out_ref):
-    picked = jnp.dot(
-        rows_ref[...], received_ref[...], preferred_element_type=jnp.float32
-    ).astype(jnp.bfloat16)
-    out_ref[0] = base_ref[0] + jnp.dot(
-        picked, columns_ref[...], preferred_element_type=jnp.float32
-    )
-
-
-def place_rows(row_pick, column_pick, received, base):
-    count, slots = row_pick.shape
-    depth = column_pick.shape[0]
+def place_kernel(maps_ref, rows_ref, received_ref, base_a, base_b, out_a, out_b, columns):
+    depth = columns.shape[1]
+
+    @pl.when((pl.program_id(0) == 0) & (pl.program_id(1) == 0))
+    def _():
+        wide = lax.broadcasted_iota(jnp.int32, (depth, depth), 0)
+        for channel in range(2):
+            hit = wide == maps_ref[channel : channel + 1, :]
+            columns[channel] = jnp.where(hit, 1.0, 0.0).astype(jnp.bfloat16)
+
+    for channel, (base, out) in enumerate(((base_a, out_a), (base_b, out_b))):
+        picked = jnp.dot(
+            rows_ref[channel], received_ref[...], preferred_element_type=jnp.float32
+        ).astype(jnp.bfloat16)
+        out[0] = base[0] + jnp.dot(picked, columns[channel], preferred_element_type=jnp.float32)
+
+
+def place_rows(col_maps, row_pick, received, base_a, base_b):
+    _, count, slots = row_pick.shape
+    depth = col_maps.shape[1]
+    block = pl.BlockSpec((1, count // 2, depth), lambda part, half: (part, half, 0))
     return pl.pallas_call(
         place_kernel,
-        out_shape=jax.ShapeDtypeStruct((2, count, depth), jnp.float32),
-        grid=(2,),
+        out_shape=[jax.ShapeDtypeStruct((2, count, depth), jnp.float32)] * 2,
+        grid=(2, 2),
         in_specs=[
-            pl.BlockSpec((count, slots), lambda part: (0, 0)),
-            pl.BlockSpec((depth, depth), lambda part: (0, 0)),
-            pl.BlockSpec((slots, depth), lambda part: (0, part)),
-            pl.BlockSpec((1, count, depth), lambda part: (part, 0, 0)),
+            pl.BlockSpec((2, depth), lambda part, half: (0, 0)),
+            pl.BlockSpec((2, count // 2, slots), lambda part, half: (0, half, 0)),
+            pl.BlockSpec((slots, depth), lambda part, half: (0, part)),
+            block,
+            block,
         ],
-        out_specs=pl.BlockSpec((1, count, depth), lambda part: (part, 0, 0)),
+        out_specs=[block, block],
+        scratch_shapes=[pltpu.VMEM((2, depth, depth), jnp.bfloat16)],
         cost_estimate=pl.CostEstimate(
-            flops=4 * count * depth * (slots + depth),
-            bytes_accessed=16 * count * depth + 2 * depth * depth,
+            flops=8 * count * depth * (slots + depth),
+            bytes_accessed=32 * count * depth,
             transcendentals=0,
         ),
         name="place_rows",
-    )(row_pick, column_pick, received, base)
+    )(col_maps, row_pick, received, base_a, base_b)
 
 
 def per_device(vertex_ladder, vertex_cross_a, vertex_cross_b, bubble, row_maps, col_maps):
@@ -190,10 +204,9 @@
     def move(value, target):
         return lax.ppermute(value, ("pb", "ka"), [(i, target(i)) for i in range(dev_count)])
 
-    gamma_low = vertex_ladder.astype(jnp.bfloat16)
-
     def piece_of(index):
-        return lax.dynamic_index_in_dim(gamma_low, index, 1, keepdims=False)
+        piece = lax.dynamic_index_in_dim(vertex_ladder, index, 1, keepdims=False)
+        return piece.astype(jnp.bfloat16)
 
     held = {}
     for d in range(q_local):
@@ -264,19 +277,23 @@
     reducible = jnp.take(stacked, order, axis=0).astype(jnp.float32)
     ladder_out = vertex_ladder + jnp.moveaxis(reducible, 0, 1)
 
-    crossed = []
-    for channel, base in ((0, vertex_cross_a), (1, vertex_cross_b)):
+    row_pick = []
+    for channel in range(2):
         source_dev, slot_index = slots_of(tables[channel])
         slot = (source_dev * 2 + channel) * per_peer + slot_index
-        row_pick = (
-            slot[:, None] == jnp.arange(dev_count * 2 * per_peer, dtype=jnp.int32)[None, :]
-        ).astype(jnp.bfloat16)
-        column_pick = (
-            jnp.arange(col_count, dtype=jnp.int32)[:, None] == col_maps[channel][None, :]
-        ).astype(jnp.bfloat16)
-        placed = place_rows(row_pick, column_pick, received, base.reshape(2, local_count, col_count))
-        crossed.append(placed.reshape(base.shape))
-    return (ladder_out, crossed[0], crossed[1])
+        row_pick.append(slot[:, None] == jnp.arange(dev_count * 2 * per_peer, dtype=jnp.int32))
+    crossed_a, crossed_b = place_rows(
+        col_maps,
+        jnp.stack(row_pick).astype(jnp.bfloat16),
+        received,
+        vertex_cross_a.reshape(2, local_count, col_count),
+        vertex_cross_b.reshape(2, local_count, col_count),
+    )
+    return (
+        ladder_out,
+        crossed_a.reshape(vertex_cross_a.shape),
+        crossed_b.reshape(vertex_cross_b.shape),
+    )
 
 
 def parts_of(q_local):

time: 173 us -> 167 us (0.965)
  other arithmetic: 16.9 us -> 8.9 us
  waiting for transfers between devices: 76.3 us -> 82.5 us
  Pallas kernels: 35.8 us -> 32.3 us
    convert_element_type x5 -> x1, other arithmetic: 7.84 us -> 0.86 us  [per_device(): jnp.stack(row_pick).astype(jnp.bfloat16)]
    all_to_all x1, waiting for transfers between devices: 34.2 us -> 39.8 us  [per_device(): lax.all_to_all(send.reshape(dev_count, 2 * per_peer, 2 * col_count), ('pb...]
    pallas_call x2 -> x1, Pallas kernels: 10.6 us -> 8.4 us  [place_rows(): pl.pallas_call(place_kernel, out_shape=[jax.ShapeDtypeStruct((2, count, d...]
    unnamed x48 -> x32, local copies, waits for them, and re-layouts: 3.77 us -> 1.65 us
  transfers between devices with their start and end apart: 25 -> 25, of which waited for: 9 -> 9; matrix products, arithmetic and copies ran while one was open for 11% -> 8% of each run, Pallas kernels for 6% -> 7%
where the time goes in v1:
time: 167 us
  waiting for transfers between devices  82.5 us (49%)
  starting transfers between devices  35.7 us (21%)
  Pallas kernels  32.3 us (19%)
  other arithmetic  8.9 us (5%)
  local copies, waits for them, and re-layouts  6.46 us (4%)
    ppermute x24, waiting for transfers between devices, move(): lax.ppermute(value, ('pb', 'ka'), [(i, target(i)) for i in range(dev_coun...  42.7 us
    all_to_all x1, waiting for transfers between devices, per_device(): lax.all_to_all(send.reshape(dev_count, 2 * per_peer, 2 * col_count), ('pb...  39.8 us
    ppermute x24, starting transfers between devices, move(): lax.ppermute(value, ('pb', 'ka'), [(i, target(i)) for i in range(dev_coun...  27 us
    pallas_call x2, Pallas kernels, ladder(): pl.pallas_call(functools.partial(ladder_kernel, groups, low_count, wanted...  21.9 us
    all_to_all x1, starting transfers between devices, per_device(): lax.all_to_all(send.reshape(dev_count, 2 * per_peer, 2 * col_count), ('pb...  8.67 us
    pallas_call x1, Pallas kernels, place_rows(): pl.pallas_call(place_kernel, out_shape=[jax.ShapeDtypeStruct((2, count, d...  8.4 us
  transfers between devices with their start and end apart: 25, of which 9 were waited for; matrix products, arithmetic and copies ran while one was open for 8% of the time, Pallas kernels for 7%

profile of v1, /device:TPU:0, one launch (start us, length us, event | category | flops | bytes accessed | tf_op | source)
XLA Modules:
  0.0 167.0 jit_solution(7384079099932641573)
XLA Ops:
  0.7 1.7 %fusion.4 = (bf16[2,64,1024]{2,1,0:T(8,128)(2,1)S(1)}, bf16[2,64,1024]{2,1,0:T(8,128)(2,1)S(1)}, bf16[2,64,1024]{2,1,0:T(8,128)(2,1)S(1)}, bf16[2,64,1024]{2,1,0:T(8,128)(2,1)S(1)}) fusion(s32[]{:T(128)S(6)} %select_n.423, s32[]{:T(128)S(6)} %select_n.422, s32[]{:T(128)S(6)} %select_n.421, s32[]{:T(128)S(6)} %select_n.419, f32[2,4,64,1024]{3,2,1,0:T(8,128)} %param.6), kind=kLoop, calls=%fused_computation.15 | loop fusion | bytes 2097168 | tf_op jit(solution)/shard_map/convert_element_type | solution.py:209
  2.4 4.1 %collective-permute-start.9 = (bf16[2,64,1024]{2,1,0:T(8,128)(2,1)S(1)}, bf16[2,64,1024]{2,1,0:T(8,128)(2,1)S(1)}, u32[]{:S(2)}, u32[]{:S(2)}) collective-permute-start(bf16[2,64,1024]{2,1,0:T(8,128)(2,1)S(1)} %get-tuple-element.31), channel_id=1, source_target_pairs={{0,8},{1,9},{2,24},{3,25},{4,12},{5,13},{6,28},{7,29},{8,0},{9,1},... | collective-permute-start | bytes 786440 | tf_op jit(solution)/shard_map/ppermute | solution.py:205
  6.5 1.3 collective-permute-start.13
  7.9 0.7 collective-permute-start.1
  8.5 0.3 collective-permute-start.5
  8.9 3.5 %collective-permute-start = (f32[2,1024]{1,0:T(2,128)S(1)}, f32[2,1024]{1,0:T(2,128)S(1)}, u32[]{:S(2)}, u32[]{:S(2)}) collective-permute-start(f32[2,1024]{1,0:T(2,128)S(1)} %bitcast.104), channel_id=1, source_target_pairs={{0,16},{1,17},{2,18},{3,19},{4,20},{5,21},{6,22},{7,23},{8,24},{9,... | collective-permute-start | bytes 24584 | tf_op jit(solution)/shard_map/ppermute | solution.py:205
  12.6 0.1 reshape.844
  13.0 0.1 reshape.846
  13.1 0.1 fusion.48
  13.2 0.6 reduce-window.34
  13.8 0.1 fusion.51
  14.0 0.2 slice_reduce_fusion.1
  14.2 0.6 reduce-window.36
  14.8 0.1 fusion.15
  14.9 9.4 %collective-permute-done.9.refs_8_ = bf16[2,64,1024]{2,1,0:T(8,128)(2,1)S(1)} collective-permute-done((bf16[2,64,1024]{2,1,0:T(8,128)(2,1)S(1)}, bf16[2,64,1024]{2,1,0:T(8,128)(2,1)S(1)}, u32[]{:S(2)}, u32[]{:S(2)}) %collective-permute-start.9) | collective-permute-done | bytes 262176 | tf_op jit(solution)/shard_map/ppermute | solution.py:205
  24.3 2.1 %collective-permute-start.11 = (bf16[2,64,1024]{2,1,0:T(8,128)(2,1)S(1)}, bf16[2,64,1024]{2,1,0:T(8,128)(2,1)S(1)}, u32[]{:S(2)}, u32[]{:S(2)}) collective-permute-start(bf16[2,64,1024]{2,1,0:T(8,128)(2,1)S(1)} %collective-permute-done.9.refs_8_), channel_id=1, source_target_pairs={{0,1},{1,0},{2,3},{3,2},{4,5},{5,4},{6,7},{7,6},{8,9},{9,8},{10,11... | collective-permute-start | bytes 786440 | tf_op jit(solution)/shard_map/ppermute | solution.py:205
  26.6 0.2 slice_reduce_fusion
  26.8 0.7 collective-permute-start.10
  27.7 1.7 %collective-permute-start.3 = (bf16[2,64,1024]{2,1,0:T(8,128)(2,1)S(1)}, bf16[2,64,1024]{2,1,0:T(8,128)(2,1)S(1)}, u32[]{:S(2)}, u32[]{:S(2)}) collective-permute-start(bf16[2,64,1024]{2,1,0:T(8,128)(2,1)S(1)} %collective-permute-done.1.refs_0_), channel_id=1, source_target_pairs={{0,1},{1,0},{2,3},{3,2},{4,5},{5,4},{6,7},{7,6},{8,9},{9,8},{10,11... | collective-permute-start | bytes 786440 | tf_op jit(solution)/shard_map/ppermute | solution.py:205
  29.4 3.9 %collective-permute-done.11.refs_10_ = bf16[2,64,1024]{2,1,0:T(8,128)(2,1)S(1)} collective-permute-done((bf16[2,64,1024]{2,1,0:T(8,128)(2,1)S(1)}, bf16[2,64,1024]{2,1,0:T(8,128)(2,1)S(1)}, u32[]{:S(2)}, u32[]{:S(2)}) %collective-permute-start.11) | collective-permute-done | bytes 262176 | tf_op jit(solution)/shard_map/ppermute | solution.py:205
  33.3 0.8 collective-permute-start.2
  34.1 4.8 %collective-permute-done.15.refs_14_ = bf16[2,64,1024]{2,1,0:T(8,128)(2,1)S(1)} collective-permute-done((bf16[2,64,1024]{2,1,0:T(8,128)(2,1)S(1)}, bf16[2,64,1024]{2,1,0:T(8,128)(2,1)S(1)}, u32[]{:S(2)}, u32[]{:S(2)}) %collective-permute-start.15) | collective-permute-done | bytes 262176 | tf_op jit(solution)/shard_map/ppermute | solution.py:205
  38.9 2.4 %collective-permute-start.7 = (bf16[2,64,1024]{2,1,0:T(8,128)(2,1)S(1)}, bf16[2,64,1024]{2,1,0:T(8,128)(2,1)}, u32[]{:S(2)}, u32[]{:S(2)}) collective-permute-start(bf16[2,64,1024]{2,1,0:T(8,128)(2,1)S(1)} %collective-permute-done.5.refs_4_), channel_id=1, source_target_pairs={{0,1},{1,0},{2,3},{3,2},{4,5},{5,4},{6,7},{7,6},{8,9},{9,8},{10,11... | collective-permute-start | bytes 786440 | tf_op jit(solution)/shard_map/ppermute | solution.py:205
  41.3 0.6 multiply_reduce_fusion.1
  42.0 0.6 multiply_reduce_fusion
  42.6 1.9 %collective-permute-done.3.refs_2_ = bf16[2,64,1024]{2,1,0:T(8,128)(2,1)S(1)} collective-permute-done((bf16[2,64,1024]{2,1,0:T(8,128)(2,1)S(1)}, bf16[2,64,1024]{2,1,0:T(8,128)(2,1)S(1)}, u32[]{:S(2)}, u32[]{:S(2)}) %collective-permute-start.3) | collective-permute-done | bytes 262176 | tf_op jit(solution)/shard_map/ppermute | solution.py:205
  44.5 0.9 collective-permute-start.6
  45.4 4.8 %collective-permute-done.7.refs_6_ = bf16[2,64,1024]{2,1,0:T(8,128)(2,1)} collective-permute-done((bf16[2,64,1024]{2,1,0:T(8,128)(2,1)S(1)}, bf16[2,64,1024]{2,1,0:T(8,128)(2,1)}, u32[]{:S(2)}, u32[]{:S(2)}) %collective-permute-start.7) | collective-permute-done | bytes 262176 | tf_op jit(solution)/shard_map/ppermute | solution.py:205
  50.2 0.2 collective-permute-start.12
  50.4 0.4 collective-permute-start.16
  50.8 0.2 collective-permute-start.4
  50.9 0.4 collective-permute-start.8
  51.3 0.7 pad_add_fusion.1.place_ref
  51.9 0.6 broadcast_select_fusion.chi_ref
  52.5 0.1 collective-permute-done.4.refs_3_
  52.7 0.4 collective-permute-done.8.refs_7_
  53.1 0.1 copy-done.14
  53.2 10.9 %ladder.2 = (bf16[2,64,1024]{2,1,0:T(8,128)(2,1)}, bf16[2,64,1024]{2,1,0:T(8,128)(2,1)}) custom-call(s32[3]{0:T(128)} %pad_add_fusion.1.place_ref, f32[2,1024]{1,0:T(2,128)} %broadcast_select_fusion.chi_ref, bf16[2,64,1024]{2,1,0:T(8,128)(2,1)} %copy-done.6, bf16[2,64,1024]{2,1,0:T(8,128)(2,1)} %copy-done.13, bf16[2,64,1024]{2,1,0:T(8,128)(2,1)} %copy-done.12, ...), custom_call_target="tpu_custom_call" | custom-call | flops 6442450944 | bytes 5242880 | tf_op jit(solution)/shard_map/ladder/pallas_call | solution.py:89
  64.1 1.1 collective-permute-start.18
  65.2 11.1 %ladder.3 = (bf16[2,64,1024]{2,1,0:T(8,128)(2,1)}, bf16[2,64,1024]{2,1,0:T(8,128)(2,1)}) custom-call(s32[3]{0:T(128)} %pad_add_fusion.1.place_ref, f32[2,1024]{1,0:T(2,128)} %broadcast_select_fusion.chi_ref, bf16[2,64,1024]{2,1,0:T(8,128)(2,1)} %copy-done.6, bf16[2,64,1024]{2,1,0:T(8,128)(2,1)} %copy-done.13, bf16[2,64,1024]{2,1,0:T(8,128)(2,1)} %copy-done.12, ...), custom_call_target="tpu_custom_call" | custom-call | flops 6442450944 | bytes 5242880 | tf_op jit(solution)/shard_map/ladder/pallas_call | solution.py:89
  76.3 3.0 %collective-permute-start.20 = (bf16[2,64,1024]{2,1,0:T(8,128)(2,1)}, bf16[2,64,1024]{2,1,0:T(8,128)(2,1)S(1)}, u32[]{:S(2)}, u32[]{:S(2)}) collective-permute-start(bf16[2,64,1024]{2,1,0:T(8,128)(2,1)} %get-tuple-element.11), channel_id=1, source_target_pairs={{0,8},{1,9},{2,10},{3,11},{4,12},{5,13},{6,14},{7,15},{8,0},{9,1},... | collective-permute-start | bytes 786440 | tf_op jit(solution)/shard_map/ppermute | solution.py:205
  79.3 0.4 collective-permute-start.22
  79.7 0.1 eq.208
  79.8 0.1 fusion.chosen_ref
  80.0 17.3 %collective-permute-done.20.refs_2_ = bf16[2,64,1024]{2,1,0:T(8,128)(2,1)S(1)} collective-permute-done((bf16[2,64,1024]{2,1,0:T(8,128)(2,1)}, bf16[2,64,1024]{2,1,0:T(8,128)(2,1)S(1)}, u32[]{:S(2)}, u32[]{:S(2)}) %collective-permute-start.20) | collective-permute-done | bytes 262176 | tf_op jit(solution)/shard_map/ppermute | solution.py:205
  97.3 2.0 %select_rows.1 = bf16[512,2048]{1,0:T(8,128)(2,1)} custom-call(bf16[512,256]{1,0:T(8,128)(2,1)S(1)} %fusion.chosen_ref, bf16[2,64,1024]{2,1,0:T(8,128)(2,1)S(1)} %copy-done.1, bf16[2,64,1024]{2,1,0:T(8,128)(2,1)S(1)} %collective-permute-done.18.refs_1_, bf16[2,64,1024]{2,1,0:T(8,128)(2,1)S(1)} %collective-permute-done.20.refs_2_, ...), custom_call_target="tpu_custom_call" | custom-call | flops 536870912 | bytes 4194304 | tf_op jit(solution)/shard_map/select_rows/pallas_call | solution.py:126
  99.3 8.7 %all-to-all-start = ((bf16[32,16,2048]{2,1,0:T(8,128)(2,1)}), bf16[32,16,2048]{2,1,0:T(8,128)(2,1)}, u32[]{:S(2)}, u32[]{:S(2)}) async-start(bf16[32,16,2048]{2,1,0:T(8,128)(2,1)} %bitcast.23), calls=%async_computation | async-start | bytes 4194304 | tf_op jit(solution)/shard_map/all_to_all | solution.py:271
  108.1 0.6 reduce-window.30
  108.7 0.2 slice_reduce_fusion.2
  108.9 0.6 reduce-window.26
  109.5 0.2 slice_reduce_fusion.3
  110.0 0.1 iota_compare_fusion.1
  110.2 0.1 iota_compare_fusion.2
  110.3 0.7 collective-permute-start.17
  111.0 0.7 collective-permute-start.19
  111.7 0.7 collective-permute-start.23
  112.4 0.7 collective-permute-start.21
  113.1 0.9 add_convert_fusion.rows_ref
  114.0 0.1 pad_maximum_fusion
  114.1 1.6 gather_fusion
  115.7 1.6 bitcast_add_fusion
  117.3 1.5 copy.99
  118.8 39.8 %all-to-all-done = bf16[32,16,2048]{2,1,0:T(8,128)(2,1)} async-done(((bf16[32,16,2048]{2,1,0:T(8,128)(2,1)}), bf16[32,16,2048]{2,1,0:T(8,128)(2,1)}, u32[]{:S(2)}, u32[]{:S(2)}) %all-to-all-start) | async-done | bytes 2097184 | tf_op jit(solution)/shard_map/all_to_all | solution.py:271
  158.6 8.4 %place_rows.1 = (f32[2,256,1024]{2,1,0:T(8,128)}, f32[2,256,1024]{2,1,0:T(8,128)}) custom-call(s32[2,1024]{1,0:T(2,128)} %maps_ref.1, bf16[2,256,512]{2,1,0:T(8,128)(2,1)} %add_convert_fusion.rows_ref, bf16[512,2048]{1,0:T(8,128)(2,1)} %bitcast.24.received_ref, f32[2,256,1024]{2,1,0:T(8,128)} %bitcast.105, f32[2,256,1024]{2,1,0:T(8,128)} %bitcast.106), custom_call_target="tpu_custom_call" | custom-call | flops 3221225472 | bytes 8388608 | tf_op jit(solution)/shard_map/place_rows/pallas_call | solution.py:160
  (81 shorter events, 1.4 us)
Async XLA Ops:
  0.6 8.2 %copy-start = (f32[2,4,1024]{2,1,0:T(4,128)S(1)}, f32[2,4,1024]{2,1,0:T(4,128)}, u32[]{:S(2)}) copy-start(f32[2,4,1024]{2,1,0:T(4,128)} %param.9) | copy-start | bytes 98308
  0.6 11.8 %copy-start.3 = (s32[2,8,1024]{2,1,0:T(8,128)S(1)}, s32[2,8,1024]{2,1,0:T(8,128)}, u32[]{:S(2)}) copy-start(s32[2,8,1024]{2,1,0:T(8,128)} %param.10) | copy-start | bytes 196612
  2.4 21.9 %collective-permute-start.9 = (bf16[2,64,1024]{2,1,0:T(8,128)(2,1)S(1)}, bf16[2,64,1024]{2,1,0:T(8,128)(2,1)S(1)}, u32[]{:S(2)}, u32[]{:S(2)}) collective-permute-start(bf16[2,64,1024]{2,1,0:T(8,128)(2,1)S(1)} %get-tuple-element.31), channel_id=1, source_target_pairs={{0,8},{1,9},{2,24},{3,25},{4,12},{5,13},{6,28},{7,29},{8,0},{9,1},... | collective-permute-start | bytes 786440 | tf_op jit(solution)/shard_map/ppermute | solution.py:205
  6.5 19.9 %collective-permute-start.13 = (bf16[2,64,1024]{2,1,0:T(8,128)(2,1)S(1)}, bf16[2,64,1024]{2,1,0:T(8,128)(2,1)S(1)}, u32[]{:S(2)}, u32[]{:S(2)}) collective-permute-start(bf16[2,64,1024]{2,1,0:T(8,128)(2,1)S(1)} %get-tuple-element.30), channel_id=1, source_target_pairs={{0,12},{1,13},{2,28},{3,29},{4,8},{5,9},{6,24},{7,25},{8,4},{9,5},... | collective-permute-start | bytes 786440 | tf_op jit(solution)/shard_map/ppermute | solution.py:205
  7.9 19.7 %collective-permute-start.1 = (bf16[2,64,1024]{2,1,0:T(8,128)(2,1)S(1)}, bf16[2,64,1024]{2,1,0:T(8,128)(2,1)S(1)}, u32[]{:S(2)}, u32[]{:S(2)}) collective-permute-start(bf16[2,64,1024]{2,1,0:T(8,128)(2,1)S(1)} %get-tuple-element.33), channel_id=1, source_target_pairs={{0,0},{1,1},{2,16},{3,17},{4,4},{5,5},{6,20},{7,21},{8,8},{9,9},{1... | collective-permute-start | bytes 786440 | tf_op jit(solution)/shard_map/ppermute | solution.py:205
  8.5 19.1 %collective-permute-start.5 = (bf16[2,64,1024]{2,1,0:T(8,128)(2,1)S(1)}, bf16[2,64,1024]{2,1,0:T(8,128)(2,1)S(1)}, u32[]{:S(2)}, u32[]{:S(2)}) collective-permute-start(bf16[2,64,1024]{2,1,0:T(8,128)(2,1)S(1)} %get-tuple-element.32), channel_id=1, source_target_pairs={{0,4},{1,5},{2,20},{3,21},{4,0},{5,1},{6,16},{7,17},{8,12},{9,13},... | collective-permute-start | bytes 786440 | tf_op jit(solution)/shard_map/ppermute | solution.py:205
  8.9 18.0 %collective-permute-start = (f32[2,1024]{1,0:T(2,128)S(1)}, f32[2,1024]{1,0:T(2,128)S(1)}, u32[]{:S(2)}, u32[]{:S(2)}) collective-permute-start(f32[2,1024]{1,0:T(2,128)S(1)} %bitcast.104), channel_id=1, source_target_pairs={{0,16},{1,17},{2,18},{3,19},{4,20},{5,21},{6,22},{7,23},{8,24},{9,... | collective-permute-start | bytes 24584 | tf_op jit(solution)/shard_map/ppermute | solution.py:205
  24.3 28.7 %copy-start.4 = (bf16[2,64,1024]{2,1,0:T(8,128)(2,1)}, bf16[2,64,1024]{2,1,0:T(8,128)(2,1)S(1)}, u32[]{:S(2)}) copy-start(bf16[2,64,1024]{2,1,0:T(8,128)(2,1)S(1)} %collective-permute-done.9.refs_8_) | copy-start | bytes 786436
  24.3 9.0 %collective-permute-start.11 = (bf16[2,64,1024]{2,1,0:T(8,128)(2,1)S(1)}, bf16[2,64,1024]{2,1,0:T(8,128)(2,1)S(1)}, u32[]{:S(2)}, u32[]{:S(2)}) collective-permute-start(bf16[2,64,1024]{2,1,0:T(8,128)(2,1)S(1)} %collective-permute-done.9.refs_8_), channel_id=1, source_target_pairs={{0,1},{1,0},{2,3},{3,2},{4,5},{5,4},{6,7},{7,6},{8,9},{9,8},{10,11... | collective-permute-start | bytes 786440 | tf_op jit(solution)/shard_map/ppermute | solution.py:205
  26.5 26.6 %copy-start.5 = (bf16[2,64,1024]{2,1,0:T(8,128)(2,1)}, bf16[2,64,1024]{2,1,0:T(8,128)(2,1)S(1)}, u32[]{:S(2)}) copy-start(bf16[2,64,1024]{2,1,0:T(8,128)(2,1)S(1)} %collective-permute-done.13.refs_12_) | copy-start | bytes 786436
  26.5 12.4 %collective-permute-start.15 = (bf16[2,64,1024]{2,1,0:T(8,128)(2,1)S(1)}, bf16[2,64,1024]{2,1,0:T(8,128)(2,1)S(1)}, u32[]{:S(2)}, u32[]{:S(2)}) collective-permute-start(bf16[2,64,1024]{2,1,0:T(8,128)(2,1)S(1)} %collective-permute-done.13.refs_12_), channel_id=1, source_target_pairs={{0,1},{1,0},{2,3},{3,2},{4,5},{5,4},{6,7},{7,6},{8,9},{9,8},{10,11... | collective-permute-start | bytes 786440 | tf_op jit(solution)/shard_map/ppermute | solution.py:205
  26.8 23.6 %collective-permute-start.10 = (bf16[2,64,1024]{2,1,0:T(8,128)(2,1)S(1)}, bf16[2,64,1024]{2,1,0:T(8,128)(2,1)S(1)}, u32[]{:S(2)}, u32[]{:S(2)}) collective-permute-start(bf16[2,64,1024]{2,1,0:T(8,128)(2,1)S(1)} %collective-permute-done.9.refs_8_), channel_id=1, source_target_pairs={{0,16},{1,17},{2,18},{3,19},{4,20},{5,21},{6,22},{7,23},{8,24},{9,... | collective-permute-start | bytes 786440 | tf_op jit(solution)/shard_map/ppermute | solution.py:205
  27.6 25.5 %copy-start.6 = (bf16[2,64,1024]{2,1,0:T(8,128)(2,1)}, bf16[2,64,1024]{2,1,0:T(8,128)(2,1)S(1)}, u32[]{:S(2)}) copy-start(bf16[2,64,1024]{2,1,0:T(8,128)(2,1)S(1)} %collective-permute-done.1.refs_0_) | copy-start | bytes 786436
  27.6 23.2 %collective-permute-start.14 = (bf16[2,64,1024]{2,1,0:T(8,128)(2,1)S(1)}, bf16[2,64,1024]{2,1,0:T(8,128)(2,1)S(1)}, u32[]{:S(2)}, u32[]{:S(2)}) collective-permute-start(bf16[2,64,1024]{2,1,0:T(8,128)(2,1)S(1)} %collective-permute-done.13.refs_12_), channel_id=1, source_target_pairs={{0,16},{1,17},{2,18},{3,19},{4,20},{5,21},{6,22},{7,23},{8,24},{9,... | collective-permute-start | bytes 786440 | tf_op jit(solution)/shard_map/ppermute | solution.py:205
  27.7 25.4 %copy-start.7 = (bf16[2,64,1024]{2,1,0:T(8,128)(2,1)}, bf16[2,64,1024]{2,1,0:T(8,128)(2,1)S(1)}, u32[]{:S(2)}) copy-start(bf16[2,64,1024]{2,1,0:T(8,128)(2,1)S(1)} %collective-permute-done.5.refs_4_) | copy-start | bytes 786436
  27.7 16.8 %collective-permute-start.3 = (bf16[2,64,1024]{2,1,0:T(8,128)(2,1)S(1)}, bf16[2,64,1024]{2,1,0:T(8,128)(2,1)S(1)}, u32[]{:S(2)}, u32[]{:S(2)}) collective-permute-start(bf16[2,64,1024]{2,1,0:T(8,128)(2,1)S(1)} %collective-permute-done.1.refs_0_), channel_id=1, source_target_pairs={{0,1},{1,0},{2,3},{3,2},{4,5},{5,4},{6,7},{7,6},{8,9},{9,8},{10,11... | collective-permute-start | bytes 786440 | tf_op jit(solution)/shard_map/ppermute | solution.py:205
  33.3 19.8 %copy-start.8 = (bf16[2,64,1024]{2,1,0:T(8,128)(2,1)}, bf16[2,64,1024]{2,1,0:T(8,128)(2,1)S(1)}, u32[]{:S(2)}) copy-start(bf16[2,64,1024]{2,1,0:T(8,128)(2,1)S(1)} %collective-permute-done.11.refs_10_) | copy-start | bytes 786436
  33.3 17.6 %collective-permute-start.2 = (bf16[2,64,1024]{2,1,0:T(8,128)(2,1)S(1)}, bf16[2,64,1024]{2,1,0:T(8,128)(2,1)S(1)}, u32[]{:S(2)}, u32[]{:S(2)}) collective-permute-start(bf16[2,64,1024]{2,1,0:T(8,128)(2,1)S(1)} %collective-permute-done.1.refs_0_), channel_id=1, source_target_pairs={{0,16},{1,17},{2,18},{3,19},{4,20},{5,21},{6,22},{7,23},{8,24},{9,... | collective-permute-start | bytes 786440 | tf_op jit(solution)/shard_map/ppermute | solution.py:205
  38.9 14.2 %copy-start.9 = (bf16[2,64,1024]{2,1,0:T(8,128)(2,1)}, bf16[2,64,1024]{2,1,0:T(8,128)(2,1)S(1)}, u32[]{:S(2)}) copy-start(bf16[2,64,1024]{2,1,0:T(8,128)(2,1)S(1)} %collective-permute-done.15.refs_14_) | copy-start | bytes 786436
  38.9 11.3 %collective-permute-start.7 = (bf16[2,64,1024]{2,1,0:T(8,128)(2,1)S(1)}, bf16[2,64,1024]{2,1,0:T(8,128)(2,1)}, u32[]{:S(2)}, u32[]{:S(2)}) collective-permute-start(bf16[2,64,1024]{2,1,0:T(8,128)(2,1)S(1)} %collective-permute-done.5.refs_4_), channel_id=1, source_target_pairs={{0,1},{1,0},{2,3},{3,2},{4,5},{5,4},{6,7},{7,6},{8,9},{9,8},{10,11... | collective-permute-start | bytes 786440 | tf_op jit(solution)/shard_map/ppermute | solution.py:205
  44.5 8.6 %copy-start.12 = (bf16[2,64,1024]{2,1,0:T(8,128)(2,1)}, bf16[2,64,1024]{2,1,0:T(8,128)(2,1)S(1)}, u32[]{:S(2)}) copy-start(bf16[2,64,1024]{2,1,0:T(8,128)(2,1)S(1)} %collective-permute-done.3.refs_2_) | copy-start | bytes 786436
  44.5 8.0 %collective-permute-start.6 = (bf16[2,64,1024]{2,1,0:T(8,128)(2,1)S(1)}, bf16[2,64,1024]{2,1,0:T(8,128)(2,1)S(1)}, u32[]{:S(2)}, u32[]{:S(2)}) collective-permute-start(bf16[2,64,1024]{2,1,0:T(8,128)(2,1)S(1)} %collective-permute-done.5.refs_4_), channel_id=1, source_target_pairs={{0,16},{1,17},{2,18},{3,19},{4,20},{5,21},{6,22},{7,23},{8,24},{9,... | collective-permute-start | bytes 786440 | tf_op jit(solution)/shard_map/ppermute | solution.py:205
  50.2 2.3 %collective-permute-start.12 = (bf16[2,64,1024]{2,1,0:T(8,128)(2,1)S(1)}, bf16[2,64,1024]{2,1,0:T(8,128)(2,1)}, u32[]{:S(2)}, u32[]{:S(2)}) collective-permute-start(bf16[2,64,1024]{2,1,0:T(8,128)(2,1)S(1)} %collective-permute-done.11.refs_10_), channel_id=1, source_target_pairs={{0,16},{1,17},{2,18},{3,19},{4,20},{5,21},{6,22},{7,23},{8,24},{9,... | collective-permute-start | bytes 786440 | tf_op jit(solution)/shard_map/ppermute | solution.py:205
  50.4 2.7 %copy-start.10 = (bf16[2,64,1024]{2,1,0:T(8,128)(2,1)}, bf16[2,64,1024]{2,1,0:T(8,128)(2,1)S(1)}, u32[]{:S(2)}) copy-start(bf16[2,64,1024]{2,1,0:T(8,128)(2,1)S(1)} %collective-permute-done.10.refs_9_) | copy-start | bytes 786436
  50.4 2.1 %collective-permute-start.16 = (bf16[2,64,1024]{2,1,0:T(8,128)(2,1)S(1)}, bf16[2,64,1024]{2,1,0:T(8,128)(2,1)}, u32[]{:S(2)}, u32[]{:S(2)}) collective-permute-start(bf16[2,64,1024]{2,1,0:T(8,128)(2,1)S(1)} %collective-permute-done.15.refs_14_), channel_id=1, source_target_pairs={{0,16},{1,17},{2,18},{3,19},{4,20},{5,21},{6,22},{7,23},{8,24},{9,... | collective-permute-start | bytes 786440 | tf_op jit(solution)/shard_map/ppermute | solution.py:205
  50.8 2.3 %copy-start.11 = (bf16[2,64,1024]{2,1,0:T(8,128)(2,1)}, bf16[2,64,1024]{2,1,0:T(8,128)(2,1)S(1)}, u32[]{:S(2)}) copy-start(bf16[2,64,1024]{2,1,0:T(8,128)(2,1)S(1)} %collective-permute-done.14.refs_13_) | copy-start | bytes 786436
  50.8 1.9 %collective-permute-start.4 = (bf16[2,64,1024]{2,1,0:T(8,128)(2,1)S(1)}, bf16[2,64,1024]{2,1,0:T(8,128)(2,1)}, u32[]{:S(2)}, u32[]{:S(2)}) collective-permute-start(bf16[2,64,1024]{2,1,0:T(8,128)(2,1)S(1)} %collective-permute-done.3.refs_2_), channel_id=1, source_target_pairs={{0,16},{1,17},{2,18},{3,19},{4,20},{5,21},{6,22},{7,23},{8,24},{9,... | collective-permute-start | bytes 786440 | tf_op jit(solution)/shard_map/ppermute | solution.py:205
  50.9 2.2 %copy-start.13 = (bf16[2,64,1024]{2,1,0:T(8,128)(2,1)}, bf16[2,64,1024]{2,1,0:T(8,128)(2,1)S(1)}, u32[]{:S(2)}) copy-start(bf16[2,64,1024]{2,1,0:T(8,128)(2,1)S(1)} %collective-permute-done.2.refs_1_) | copy-start | bytes 786436
  50.9 2.1 %collective-permute-start.8 = (bf16[2,64,1024]{2,1,0:T(8,128)(2,1)}, bf16[2,64,1024]{2,1,0:T(8,128)(2,1)}, u32[]{:S(2)}, u32[]{:S(2)}) collective-permute-start(bf16[2,64,1024]{2,1,0:T(8,128)(2,1)} %collective-permute-done.7.refs_6_), channel_id=1, source_target_pairs={{0,16},{1,17},{2,18},{3,19},{4,20},{5,21},{6,22},{7,23},{8,24},{9,... | collective-permute-start | bytes 786440 | tf_op jit(solution)/shard_map/ppermute | solution.py:205
  52.5 0.7 copy-start.14
  64.1 33.2 %copy-start.1 = (bf16[2,64,1024]{2,1,0:T(8,128)(2,1)S(1)}, bf16[2,64,1024]{2,1,0:T(8,128)(2,1)}, u32[]{:S(2)}) copy-start(bf16[2,64,1024]{2,1,0:T(8,128)(2,1)} %get-tuple-element.9.refs_0_) | copy-start | bytes 786436
  64.1 15.9 %collective-permute-start.18 = (bf16[2,64,1024]{2,1,0:T(8,128)(2,1)}, bf16[2,64,1024]{2,1,0:T(8,128)(2,1)S(1)}, u32[]{:S(2)}, u32[]{:S(2)}) collective-permute-start(bf16[2,64,1024]{2,1,0:T(8,128)(2,1)} %get-tuple-element.10), channel_id=1, source_target_pairs={{0,4},{1,5},{2,6},{3,7},{4,0},{5,1},{6,2},{7,3},{8,12},{9,13},{10,... | collective-permute-start | bytes 786440 | tf_op jit(solution)/shard_map/ppermute | solution.py:205
  76.3 21.0 %collective-permute-start.20 = (bf16[2,64,1024]{2,1,0:T(8,128)(2,1)}, bf16[2,64,1024]{2,1,0:T(8,128)(2,1)S(1)}, u32[]{:S(2)}, u32[]{:S(2)}) collective-permute-start(bf16[2,64,1024]{2,1,0:T(8,128)(2,1)} %get-tuple-element.11), channel_id=1, source_target_pairs={{0,8},{1,9},{2,10},{3,11},{4,12},{5,13},{6,14},{7,15},{8,0},{9,1},... | collective-permute-start | bytes 786440 | tf_op jit(solution)/shard_map/ppermute | solution.py:205
  79.3 18.0 %collective-permute-start.22 = (bf16[2,64,1024]{2,1,0:T(8,128)(2,1)}, bf16[2,64,1024]{2,1,0:T(8,128)(2,1)S(1)}, u32[]{:S(2)}, u32[]{:S(2)}) collective-permute-start(bf16[2,64,1024]{2,1,0:T(8,128)(2,1)} %get-tuple-element.12), channel_id=1, source_target_pairs={{0,12},{1,13},{2,14},{3,15},{4,8},{5,9},{6,10},{7,11},{8,4},{9,5},... | collective-permute-start | bytes 786440 | tf_op jit(solution)/shard_map/ppermute | solution.py:205
  99.3 59.3 %all-to-all-start = ((bf16[32,16,2048]{2,1,0:T(8,128)(2,1)}), bf16[32,16,2048]{2,1,0:T(8,128)(2,1)}, u32[]{:S(2)}, u32[]{:S(2)}) async-start(bf16[32,16,2048]{2,1,0:T(8,128)(2,1)} %bitcast.23), calls=%async_computation | async-start | bytes 4194304 | tf_op jit(solution)/shard_map/all_to_all | solution.py:271
  110.3 3.6 %collective-permute-start.17 = (bf16[2,64,1024]{2,1,0:T(8,128)(2,1)S(1)}, bf16[2,64,1024]{2,1,0:T(8,128)(2,1)S(1)}, u32[]{:S(2)}, u32[]{:S(2)}) collective-permute-start(bf16[2,64,1024]{2,1,0:T(8,128)(2,1)S(1)} %copy-done.1), channel_id=1, source_target_pairs={{0,0},{1,1},{2,16},{3,17},{4,4},{5,5},{6,20},{7,21},{8,8},{9,9},{1... | collective-permute-start | bytes 786440 | tf_op jit(solution)/shard_map/ppermute | solution.py:205
  111.0 2.9 %collective-permute-start.19 = (bf16[2,64,1024]{2,1,0:T(8,128)(2,1)S(1)}, bf16[2,64,1024]{2,1,0:T(8,128)(2,1)S(1)}, u32[]{:S(2)}, u32[]{:S(2)}) collective-permute-start(bf16[2,64,1024]{2,1,0:T(8,128)(2,1)S(1)} %collective-permute-done.18.refs_1_), channel_id=1, source_target_pairs={{0,0},{1,1},{2,16},{3,17},{4,4},{5,5},{6,20},{7,21},{8,8},{9,9},{1... | collective-permute-start | bytes 786440 | tf_op jit(solution)/shard_map/ppermute | solution.py:205
  111.7 2.3 %collective-permute-start.23 = (bf16[2,64,1024]{2,1,0:T(8,128)(2,1)S(1)}, bf16[2,64,1024]{2,1,0:T(8,128)(2,1)S(1)}, u32[]{:S(2)}, u32[]{:S(2)}) collective-permute-start(bf16[2,64,1024]{2,1,0:T(8,128)(2,1)S(1)} %collective-permute-done.22.refs_3_), channel_id=1, source_target_pairs={{0,0},{1,1},{2,16},{3,17},{4,4},{5,5},{6,20},{7,21},{8,8},{9,9},{1... | collective-permute-start | bytes 786440 | tf_op jit(solution)/shard_map/ppermute | solution.py:205
  112.4 1.6 collective-permute-start.21
  114.0 1.7 %copy-start.2 = (f32[2,4,64,1024]{3,2,1,0:T(8,128)S(1)}, f32[2,4,64,1024]{3,2,1,0:T(8,128)}, u32[]{:S(2)}) copy-start(f32[2,4,64,1024]{3,2,1,0:T(8,128)} %param.6) | copy-start | bytes 6291460

commit v2 on v1

--- a/solution.py
+++ b/solution.py
@@ -11,43 +11,20 @@
 LADDER = 6
 TILE = 256
 MIB = 1 << 20
+LADDER_VMEM = 20 * MIB
+TOTAL_VMEM = 10 * MIB
 SELECT_VMEM = 14 * MIB
 
 
-def ladder_kernel(groups, low_count, wanted, place_ref, chi_ref, *refs):
-    total = groups * low_count * 2
-    pieces = refs[:total]
-    outs = refs[total : total + len(wanted)]
-    right, left, base, sems = refs[total + len(wanted) :]
-    rows = pieces[0].shape[1]
-    depth = pieces[0].shape[2]
+def ladder_steps(groups, low_count, wanted, place_ref, chi_ref, right, outs, left, base):
+    depth = right.shape[1]
+    rows = depth // (groups * low_count * 2)
     count = len(wanted) * rows
-    plane = 2 * low_count
-    group, low, core = place_ref[0], place_ref[1], place_ref[2]
-
-    def start_of(d, e, c):
-        member = lax.bitwise_xor(core, c) * low_count + lax.bitwise_xor(low, e)
-        return pl.multiple_of((lax.bitwise_xor(group, d) * plane + member) * rows, rows)
-
-    copies = []
-    for d in range(groups):
-        for e in range(low_count):
-            for c in range(2):
-                number = (d * low_count + e) * 2 + c
-                for part in range(2):
-                    copy = pltpu.make_async_copy(
-                        pieces[number].at[part],
-                        right.at[pl.ds(part * depth + start_of(d, e, c), rows), :],
-                        sems.at[number * 2 + part],
-                    )
-                    copy.start()
-                    copies.append(copy)
-    for copy in copies:
-        copy.wait()
     for i, d in enumerate(wanted):
+        start = start_of(low_count, rows, place_ref, d, 0, 0)
         for part in range(2):
             base[pl.ds(part * count + i * rows, rows), :] = right[
-                pl.ds(part * depth + start_of(d, 0, 0), rows), :
+                pl.ds(part * depth + start, rows), :
             ]
 
     def scaled(slot, columns, real, imag):
@@ -82,32 +59,62 @@
                         outs[i][part, :, columns] = rounded[start : start + rows]
 
 
-def ladder(place, chi, pieces, groups, low_count, wanted):
+def start_of(low_count, rows, place_ref, d, e, c):
+    member = lax.bitwise_xor(place_ref[2], c) * low_count + lax.bitwise_xor(place_ref[1], e)
+    return pl.multiple_of(
+        (lax.bitwise_xor(place_ref[0], d) * 2 * low_count + member) * rows, rows
+    )
+
+
+def first_kernel(groups, low_count, wanted, place_ref, chi_ref, *refs):
+    total = groups * low_count * 2
+    pieces = refs[:total]
+    outs = refs[total : total + len(wanted)]
+    right, left, base = refs[total + len(wanted) :]
+    rows, depth = pieces[0].shape[1:]
+    for d in range(groups):
+        for e in range(low_count):
+            for c in range(2):
+                piece = pieces[(d * low_count + e) * 2 + c]
+                start = start_of(low_count, rows, place_ref, d, e, c)
+                for part in range(2):
+                    right[pl.ds(part * depth + start, rows), :] = piece[part]
+    ladder_steps(groups, low_count, wanted, place_ref, chi_ref, right, outs, left, base)
+
+
+def next_kernel(groups, low_count, wanted, place_ref, chi_ref, right, *refs):
+    outs = refs[: len(wanted)]
+    left, base = refs[len(wanted) :]
+    ladder_steps(groups, low_count, wanted, place_ref, chi_ref, right, outs, left, base)
+
+
+def ladder(place, chi, pieces, right, groups, low_count, wanted):
     _, rows, depth = pieces[0].shape
     count = len(wanted) * rows
     total = groups * low_count * 2
+    vmem = pl.BlockSpec(memory_space=pltpu.VMEM)
+    first = right is None
+    shapes = [jax.ShapeDtypeStruct((2, rows, depth), jnp.bfloat16)] * len(wanted)
+    if first:
+        shapes.append(jax.ShapeDtypeStruct((2 * depth, depth), jnp.bfloat16))
     return pl.pallas_call(
-        functools.partial(ladder_kernel, groups, low_count, wanted),
-        out_shape=[jax.ShapeDtypeStruct((2, rows, depth), jnp.bfloat16)] * len(wanted),
-        in_specs=[
-            pl.BlockSpec(memory_space=pltpu.SMEM),
-            pl.BlockSpec(memory_space=pltpu.VMEM),
-        ]
-        + [pl.BlockSpec(memory_space=pl.ANY)] * total,
-        out_specs=[pl.BlockSpec(memory_space=pltpu.VMEM)] * len(wanted),
+        functools.partial(first_kernel if first else next_kernel, groups, low_count, wanted),
+        out_shape=shapes,
+        in_specs=[pl.BlockSpec(memory_space=pltpu.SMEM), vmem]
+        + [vmem] * (total if first else 1),
+        out_specs=[vmem] * len(shapes),
         scratch_shapes=[
-            pltpu.VMEM((2 * depth, depth), jnp.bfloat16),
             pltpu.VMEM((2, 2 * count, 2 * depth), jnp.bfloat16),
             pltpu.VMEM((2 * count, depth), jnp.bfloat16),
-            pltpu.SemaphoreType.DMA((total * 2,)),
         ],
         cost_estimate=pl.CostEstimate(
             flops=LADDER * 8 * count * depth * depth,
-            bytes_accessed=4 * depth * depth + 8 * count * depth,
+            bytes_accessed=4 * depth * depth * first + 8 * count * depth,
             transcendentals=0,
         ),
+        compiler_params=pltpu.CompilerParams(vmem_limit_bytes=LADDER_VMEM),
         name="ladder",
-    )(place, chi, *pieces)
+    )(place, chi, *(pieces if first else [right]))
 
 
 def select_kernel(chosen_ref, *refs):
@@ -116,19 +123,22 @@
     depth = refs[0].shape[2]
     for part in range(2):
         rows = jnp.concatenate([refs[d][part] for d in range(groups)], 0)
-        out[:, part * depth : (part + 1) * depth] = jnp.dot(
-            chosen_ref[...], rows, preferred_element_type=jnp.float32
-        ).astype(jnp.bfloat16)
+        for channel in range(2):
+            start = (channel * 2 + part) * depth
+            out[:, start : start + depth] = jnp.dot(
+                chosen_ref[channel], rows, preferred_element_type=jnp.float32
+            ).astype(jnp.bfloat16)
 
 
 def select_rows(chosen, returned):
     _, _, depth = returned[0].shape
+    _, slots, count = chosen.shape
     return pl.pallas_call(
         select_kernel,
-        out_shape=jax.ShapeDtypeStruct((chosen.shape[0], 2 * depth), jnp.bfloat16),
+        out_shape=jax.ShapeDtypeStruct((slots, 4 * depth), jnp.bfloat16),
         cost_estimate=pl.CostEstimate(
-            flops=4 * chosen.shape[0] * chosen.shape[1] * depth,
-            bytes_accessed=8 * chosen.shape[0] * depth,
+            flops=8 * slots * count * depth,
+            bytes_accessed=16 * slots * depth,
             transcendentals=0,
         ),
         compiler_params=pltpu.CompilerParams(vmem_limit_bytes=SELECT_VMEM),
@@ -136,40 +146,59 @@
     )(chosen, *returned)
 
 
-def place_kernel(maps_ref, rows_ref, received_ref, base_a, base_b, out_a, out_b, columns):
+def place_kernel(maps_ref, rows_ref, got, base_a, base_b, out_a, out_b, *scratch):
+    columns, base, moved, in_sems, out_sems = scratch
     depth = columns.shape[1]
-
-    @pl.when((pl.program_id(0) == 0) & (pl.program_id(1) == 0))
-    def _():
-        wide = lax.broadcasted_iota(jnp.int32, (depth, depth), 0)
-        for channel in range(2):
-            hit = wide == maps_ref[channel : channel + 1, :]
-            columns[channel] = jnp.where(hit, 1.0, 0.0).astype(jnp.bfloat16)
-
-    for channel, (base, out) in enumerate(((base_a, out_a), (base_b, out_b))):
-        picked = jnp.dot(
-            rows_ref[channel], received_ref[...], preferred_element_type=jnp.float32
-        ).astype(jnp.bfloat16)
-        out[0] = base[0] + jnp.dot(picked, columns[channel], preferred_element_type=jnp.float32)
+    bases, outs = (base_a, base_b), (out_a, out_b)
+    arriving, leaving = {}, []
+    for channel in range(2):
+        for part in range(2):
+            copy = pltpu.make_async_copy(
+                bases[channel].at[part], base.at[channel, part], in_sems.at[channel, part]
+            )
+            copy.start()
+            arriving[channel, part] = copy
+    wide = lax.broadcasted_iota(jnp.int32, (depth, depth), 0)
+    for channel in range(2):
+        hit = wide == maps_ref[channel : channel + 1, :]
+        columns[channel] = jnp.where(hit, 1.0, 0.0).astype(jnp.bfloat16)
+    for channel in range(2):
+        for part in range(2):
+            start = (channel * 2 + part) * depth
+            picked = jnp.dot(
+                rows_ref[channel],
+                got[:, start : start + depth],
+                preferred_element_type=jnp.float32,
+            ).astype(jnp.bfloat16)
+            arriving[channel, part].wait()
+            moved[channel, part] = base[channel, part] + jnp.dot(
+                picked, columns[channel], preferred_element_type=jnp.float32
+            )
+            copy = pltpu.make_async_copy(
+                moved.at[channel, part], outs[channel].at[part], out_sems.at[channel, part]
+            )
+            copy.start()
+            leaving.append(copy)
+    for copy in leaving:
+        copy.wait()
 
 
 def place_rows(col_maps, row_pick, received, base_a, base_b):
     _, count, slots = row_pick.shape
     depth = col_maps.shape[1]
-    block = pl.BlockSpec((1, count // 2, depth), lambda part, half: (part, half, 0))
+    vmem, hbm = pl.BlockSpec(memory_space=pltpu.VMEM), pl.BlockSpec(memory_space=pltpu.HBM)
     return pl.pallas_call(
         place_kernel,
         out_shape=[jax.ShapeDtypeStruct((2, count, depth), jnp.float32)] * 2,
-        grid=(2, 2),
-        in_specs=[
-            pl.BlockSpec((2, depth), lambda part, half: (0, 0)),
-            pl.BlockSpec((2, count // 2, slots), lambda part, half: (0, half, 0)),
-            pl.BlockSpec((slots, depth), lambda part, half: (0, part)),
-            block,
-            block,
+        in_specs=[vmem, vmem, vmem, hbm, hbm],
+        out_specs=[hbm, hbm],
+        scratch_shapes=[
+            pltpu.VMEM((2, depth, depth), jnp.bfloat16),
+            pltpu.VMEM((2, 2, count, depth), jnp.float32),
+            pltpu.VMEM((2, 2, count, depth), jnp.float32),
+            pltpu.SemaphoreType.DMA((2, 2)),
+            pltpu.SemaphoreType.DMA((2, 2)),
         ],
-        out_specs=[block, block],
-        scratch_shapes=[pltpu.VMEM((2, depth, depth), jnp.bfloat16)],
         cost_estimate=pl.CostEstimate(
             flops=8 * count * depth * (slots + depth),
             bytes_accessed=32 * count * depth,
@@ -177,6 +206,46 @@
         ),
         name="place_rows",
     )(col_maps, row_pick, received, base_a, base_b)
+
+
+def total_kernel(groups, place_ref, vertex, *refs):
+    parts, out = refs[:groups], refs[groups]
+    held, in_sems, out_sems = refs[groups + 1 :]
+    arriving, leaving = [], []
+    for d in range(groups):
+        index = lax.bitwise_xor(place_ref[0], d)
+        arriving.append(
+            pltpu.make_async_copy(vertex.at[:, index], held.at[0, d], in_sems.at[d])
+        )
+        leaving.append(pltpu.make_async_copy(held.at[1, d], out.at[:, index], out_sems.at[d]))
+        arriving[d].start()
+    for d in range(groups):
+        arriving[d].wait()
+        held[1, d] = held[0, d] + parts[d][...].astype(jnp.float32)
+        leaving[d].start()
+    for d in range(groups):
+        leaving[d].wait()
+
+
+def total(place, vertex, parts):
+    groups = len(parts)
+    vmem, hbm = pl.BlockSpec(memory_space=pltpu.VMEM), pl.BlockSpec(memory_space=pltpu.HBM)
+    return pl.pallas_call(
+        functools.partial(total_kernel, groups),
+        out_shape=jax.ShapeDtypeStruct(vertex.shape, jnp.float32),
+        in_specs=[pl.BlockSpec(memory_space=pltpu.SMEM), hbm] + [vmem] * groups,
+        out_specs=hbm,
+        scratch_shapes=[
+            pltpu.VMEM((2, groups, *parts[0].shape), jnp.float32),
+            pltpu.SemaphoreType.DMA((groups,)),
+            pltpu.SemaphoreType.DMA((groups,)),
+        ],
+        cost_estimate=pl.CostEstimate(
+            flops=vertex.size, bytes_accessed=10 * vertex.size, transcendentals=0
+        ),
+        compiler_params=pltpu.CompilerParams(vmem_limit_bytes=TOTAL_VMEM),
+        name="total",
+    )(place, vertex, *parts)
 
 
 def per_device(vertex_ladder, vertex_cross_a, vertex_cross_b, bubble, row_maps, col_maps):
@@ -225,9 +294,10 @@
     other_chi = move(own_chi, lambda i: i ^ ka_count)
     chi = jnp.where(core == top, own_chi, other_chi)
     place = jnp.stack([group, low, core]).astype(jnp.int32)
-    results = {}
-    for wanted in parts_of(q_local):
-        outs = ladder(place, chi, pieces, q_local, low_count, wanted)
+    results, right = {}, None
+    for number, wanted in enumerate(parts_of(q_local)):
+        outs = ladder(place, chi, pieces, right, q_local, low_count, wanted)
+        right = outs[-1] if number == 0 else right
         for d, out in zip(wanted, outs):
             results[d] = out
     returned = [results[0]] + [
@@ -263,25 +333,20 @@
         .reshape(dev_count, local_count)
         for channel in range(2)
     ]
-    chosen = jnp.stack([chosen_of(table) for table in tables], 1).reshape(-1)
-    chosen = (chosen[:, None] == jnp.arange(local_count, dtype=jnp.int32)[None, :]).astype(
-        jnp.bfloat16
-    )
+    chosen = jnp.stack([chosen_of(table) for table in tables]).reshape(2, local_count, 1)
+    chosen = (chosen == jnp.arange(local_count, dtype=jnp.int32)).astype(jnp.bfloat16)
     send = select_rows(chosen, returned)
     received = lax.all_to_all(
-        send.reshape(dev_count, 2 * per_peer, 2 * col_count), ("pb", "ka"), 0, 0, tiled=True
-    ).reshape(dev_count * 2 * per_peer, 2 * col_count)
-
-    stacked = jnp.stack([move(returned[d], twin_of) for d in range(q_local)])
-    order = jnp.arange(q_local, dtype=jnp.int32) ^ group
-    reducible = jnp.take(stacked, order, axis=0).astype(jnp.float32)
-    ladder_out = vertex_ladder + jnp.moveaxis(reducible, 0, 1)
+        send.reshape(dev_count, per_peer, 4 * col_count), ("pb", "ka"), 0, 0, tiled=True
+    ).reshape(local_count, 4 * col_count)
+
+    ladder_out = total(place, vertex_ladder, [move(returned[d], twin_of) for d in range(q_local)])
 
     row_pick = []
     for channel in range(2):
         source_dev, slot_index = slots_of(tables[channel])
-        slot = (source_dev * 2 + channel) * per_peer + slot_index
-        row_pick.append(slot[:, None] == jnp.arange(dev_count * 2 * per_peer, dtype=jnp.int32))
+        slot = source_dev * per_peer + slot_index
+        row_pick.append(slot[:, None] == jnp.arange(local_count, dtype=jnp.int32))
     crossed_a, crossed_b = place_rows(
         col_maps,
         jnp.stack(row_pick).astype(jnp.bfloat16),
@@ -297,7 +362,7 @@
 
 
 def parts_of(q_local):
-    return [tuple(range(q_local - 1, q_local // 2 - 1, -1)), tuple(range(q_local // 2 - 1, -1, -1))]
+    return [(d,) for d in range(q_local - 1, -1, -1)]
 
 
 def solution(mesh):

time: 167 us -> 156 us (0.934)
  waiting for transfers between devices: 82.5 us -> 71.2 us
  starting transfers between devices: 35.7 us -> 41.9 us
  other arithmetic: 8.9 us -> 5.81 us
  local copies, waits for them, and re-layouts: 6.46 us -> 3.99 us
    ppermute x24, waiting for transfers between devices: 42.7 us -> 28.8 us  [move(): lax.ppermute(value, ('pb', 'ka'), [(i, target(i)) for i in range(dev_coun...]
    ppermute x24, starting transfers between devices: 27 us -> 33 us  [move(): lax.ppermute(value, ('pb', 'ka'), [(i, target(i)) for i in range(dev_coun...]
    all_to_all x1, waiting for transfers between devices: 39.8 us -> 42.4 us  [per_device(): lax.all_to_all(send.reshape(dev_count, per_peer, 4 * col_count), ('pb', '...]
    pallas_call x3 -> x6, Pallas kernels: 23.9 us -> 23.9 us  [the longest x4 19.6 us: ladder(): pl.pallas_call(functools.partial(first_kernel if first else next_kernel,...]
  transfers between devices with their start and end apart: 25 -> 25, of which waited for: 9 -> 7; matrix products, arithmetic and copies ran while one was open for 8% -> 6% of each run, Pallas kernels for 7% -> 4%
where the time goes in v2:
time: 156 us
  waiting for transfers between devices  71.2 us (46%)
  starting transfers between devices  41.9 us (27%)
  Pallas kernels  31.4 us (20%)
  other arithmetic  5.81 us (4%)
  local copies, waits for them, and re-layouts  3.99 us (3%)
    all_to_all x1, waiting for transfers between devices, per_device(): lax.all_to_all(send.reshape(dev_count, per_peer, 4 * col_count), ('pb', '...  42.4 us
    ppermute x24, starting transfers between devices, move(): lax.ppermute(value, ('pb', 'ka'), [(i, target(i)) for i in range(dev_coun...  33 us
    ppermute x24, waiting for transfers between devices, move(): lax.ppermute(value, ('pb', 'ka'), [(i, target(i)) for i in range(dev_coun...  28.8 us
    pallas_call x4, Pallas kernels, ladder(): pl.pallas_call(functools.partial(first_kernel if first else next_kernel,...  19.6 us
    all_to_all x1, starting transfers between devices, per_device(): lax.all_to_all(send.reshape(dev_count, per_peer, 4 * col_count), ('pb', '...  8.96 us
    pallas_call x1, Pallas kernels, place_rows(): pl.pallas_call(place_kernel, out_shape=[jax.ShapeDtypeStruct((2, count, d...  7.41 us
  transfers between devices with their start and end apart: 25, of which 7 were waited for; matrix products, arithmetic and copies ran while one was open for 6% of the time, Pallas kernels for 4%

profile of v2, /device:TPU:0, one launch (start us, length us, event | category | flops | bytes accessed | tf_op | source)
XLA Modules:
  0.0 155.6 jit_solution(12023144650648479408)
XLA Ops:
  0.7 0.7 copy-done
  1.4 0.6 collective-permute-start
  2.0 1.7 %fusion.4 = (bf16[2,64,1024]{2,1,0:T(8,128)(2,1)S(1)}, bf16[2,64,1024]{2,1,0:T(8,128)(2,1)S(1)}, bf16[2,64,1024]{2,1,0:T(8,128)(2,1)S(1)}, bf16[2,64,1024]{2,1,0:T(8,128)(2,1)S(1)}) fusion(f32[2,4,64,1024]{3,2,1,0:T(8,128)} %vertex.1, s32[]{:T(128)S(6)} %select_n.400, s32[]{:T(128)S(6)} %select_n.399, s32[]{:T(128)S(6)} %select_n.398, s32[]{:T(128)S(6)} %select_n.396), kind=kLoop, calls=%fused_computation.10 | loop fusion | bytes 2097168 | tf_op jit(solution)/shard_map/convert_element_type | solution.py:278
  3.7 0.7 collective-permute-start.1
  4.3 2.7 %collective-permute-start.5 = (bf16[2,64,1024]{2,1,0:T(8,128)(2,1)S(1)}, bf16[2,64,1024]{2,1,0:T(8,128)(2,1)S(1)}, u32[]{:S(2)}, u32[]{:S(2)}) collective-permute-start(bf16[2,64,1024]{2,1,0:T(8,128)(2,1)S(1)} %get-tuple-element.13), channel_id=1, source_target_pairs={{0,4},{1,5},{2,20},{3,21},{4,0},{5,1},{6,16},{7,17},{8,12},{9,13},... | collective-permute-start | bytes 786440 | tf_op jit(solution)/shard_map/ppermute | solution.py:274
  7.0 2.6 %collective-permute-start.9 = (bf16[2,64,1024]{2,1,0:T(8,128)(2,1)S(1)}, bf16[2,64,1024]{2,1,0:T(8,128)(2,1)S(1)}, u32[]{:S(2)}, u32[]{:S(2)}) collective-permute-start(bf16[2,64,1024]{2,1,0:T(8,128)(2,1)S(1)} %get-tuple-element.12), channel_id=1, source_target_pairs={{0,8},{1,9},{2,24},{3,25},{4,12},{5,13},{6,28},{7,29},{8,0},{9,1},... | collective-permute-start | bytes 786440 | tf_op jit(solution)/shard_map/ppermute | solution.py:274
  9.6 0.1 reshape_squeeze.7
  9.7 0.1 reshape.827
  9.8 0.1 reshape.831
  9.9 0.1 reshape_squeeze.6
  10.0 0.1 reshape.825
  10.1 0.1 reshape.829
  10.3 0.1 fusion.15
  10.4 0.1 fusion.51
  10.6 0.1 fusion.48
  10.7 0.6 reduce-window.36
  11.3 0.2 slice_reduce_fusion
  11.6 0.6 reduce-window.34
  12.2 0.6 multiply_reduce_fusion
  12.8 0.2 slice_reduce_fusion.1
  13.0 0.1 stack.32
  13.2 3.5 %collective-permute-start.2 = (bf16[2,64,1024]{2,1,0:T(8,128)(2,1)S(1)}, bf16[2,64,1024]{2,1,0:T(8,128)(2,1)S(1)}, u32[]{:S(2)}, u32[]{:S(2)}) collective-permute-start(bf16[2,64,1024]{2,1,0:T(8,128)(2,1)S(1)} %collective-permute-done.1.refs_0_), channel_id=1, source_target_pairs={{0,16},{1,17},{2,18},{3,19},{4,20},{5,21},{6,22},{7,23},{8,24},{9,... | collective-permute-start | bytes 786440 | tf_op jit(solution)/shard_map/ppermute | solution.py:274
  16.7 1.7 %collective-permute-start.3 = (bf16[2,64,1024]{2,1,0:T(8,128)(2,1)S(1)}, bf16[2,64,1024]{2,1,0:T(8,128)(2,1)S(1)}, u32[]{:S(2)}, u32[]{:S(2)}) collective-permute-start(bf16[2,64,1024]{2,1,0:T(8,128)(2,1)S(1)} %collective-permute-done.1.refs_0_), channel_id=1, source_target_pairs={{0,1},{1,0},{2,3},{3,2},{4,5},{5,4},{6,7},{7,6},{8,9},{9,8},{10,11... | collective-permute-start | bytes 786440 | tf_op jit(solution)/shard_map/ppermute | solution.py:274
  18.5 0.6 multiply_reduce_fusion.1
  19.1 0.1 stack.31
  19.3 0.9 collective-permute-start.7
  20.2 5.6 %collective-permute-done.13.refs_12_ = bf16[2,64,1024]{2,1,0:T(8,128)(2,1)S(1)} collective-permute-done((bf16[2,64,1024]{2,1,0:T(8,128)(2,1)S(1)}, bf16[2,64,1024]{2,1,0:T(8,128)(2,1)S(1)}, u32[]{:S(2)}, u32[]{:S(2)}) %collective-permute-start.13) | collective-permute-done | bytes 262176 | tf_op jit(solution)/shard_map/ppermute | solution.py:274
  25.8 6.6 %collective-permute-start.10 = (bf16[2,64,1024]{2,1,0:T(8,128)(2,1)S(1)}, bf16[2,64,1024]{2,1,0:T(8,128)(2,1)S(1)}, u32[]{:S(2)}, u32[]{:S(2)}) collective-permute-start(bf16[2,64,1024]{2,1,0:T(8,128)(2,1)S(1)} %collective-permute-done.9.refs_8_), channel_id=1, source_target_pairs={{0,16},{1,17},{2,18},{3,19},{4,20},{5,21},{6,22},{7,23},{8,24},{9,... | collective-permute-start | bytes 786440 | tf_op jit(solution)/shard_map/ppermute | solution.py:274
  32.4 0.5 collective-permute-start.11
  32.9 1.5 collective-permute-start.15
  34.4 0.1 fusion.chosen_ref
  34.7 2.6 %collective-permute-start.4 = (bf16[2,64,1024]{2,1,0:T(8,128)(2,1)S(1)}, bf16[2,64,1024]{2,1,0:T(8,128)(2,1)}, u32[]{:S(2)}, u32[]{:S(2)}) collective-permute-start(bf16[2,64,1024]{2,1,0:T(8,128)(2,1)S(1)} %collective-permute-done.3.refs_2_), channel_id=1, source_target_pairs={{0,16},{1,17},{2,18},{3,19},{4,20},{5,21},{6,22},{7,23},{8,24},{9,... | collective-permute-start | bytes 786440 | tf_op jit(solution)/shard_map/ppermute | solution.py:274
  37.3 4.3 %collective-permute-done.11.refs_10_ = bf16[2,64,1024]{2,1,0:T(8,128)(2,1)S(1)} collective-permute-done((bf16[2,64,1024]{2,1,0:T(8,128)(2,1)S(1)}, bf16[2,64,1024]{2,1,0:T(8,128)(2,1)S(1)}, u32[]{:S(2)}, u32[]{:S(2)}) %collective-permute-start.11) | collective-permute-done | bytes 262176 | tf_op jit(solution)/shard_map/ppermute | solution.py:274
  41.6 1.3 collective-permute-start.12
  42.9 4.3 %collective-permute-done.15.refs_14_ = bf16[2,64,1024]{2,1,0:T(8,128)(2,1)S(1)} collective-permute-done((bf16[2,64,1024]{2,1,0:T(8,128)(2,1)S(1)}, bf16[2,64,1024]{2,1,0:T(8,128)(2,1)S(1)}, u32[]{:S(2)}, u32[]{:S(2)}) %collective-permute-start.15) | collective-permute-done | bytes 262176 | tf_op jit(solution)/shard_map/ppermute | solution.py:274
  47.2 0.4 collective-permute-start.16
  47.8 1.2 collective-permute-done.16.refs_15_
  48.9 5.6 %ladder.4 = (bf16[2,64,1024]{2,1,0:T(8,128)(2,1)S(1)}, bf16[2048,1024]{1,0:T(8,128)(2,1)S(1)}) custom-call(s32[3]{0:T(128)S(1)} %pad_add_fusion.1.place_ref, f32[2,1024]{1,0:T(2,128)S(1)} %broadcast_select_fusion.chi_ref, bf16[2,64,1024]{2,1,0:T(8,128)(2,1)S(1)} %collective-permute-done.1.refs_0_, bf16[2,64,1024]{2,1,0:T(8,128)(2,1)S(1)} %collective-permute-done.2.refs_1_, ...), custom_call_target="tpu_custom_call" | custom-call | flops 3221225472 | bytes 4718592 | tf_op jit(solution)/shard_map/ladder/pallas_call | solution.py:100
  54.5 4.6 %ladder.6 = bf16[2,64,1024]{2,1,0:T(8,128)(2,1)S(1)} custom-call(s32[3]{0:T(128)S(1)} %pad_add_fusion.1.place_ref, f32[2,1024]{1,0:T(2,128)S(1)} %broadcast_select_fusion.chi_ref, bf16[2048,1024]{1,0:T(8,128)(2,1)S(1)} %get-tuple-element.7.right), custom_call_target="tpu_custom_call" | custom-call | flops 3221225472 | bytes 524288 | tf_op jit(solution)/shard_map/ladder/pallas_call | solution.py:100
  59.1 4.8 %ladder.7 = bf16[2,64,1024]{2,1,0:T(8,128)(2,1)S(1)} custom-call(s32[3]{0:T(128)S(1)} %pad_add_fusion.1.place_ref, f32[2,1024]{1,0:T(2,128)S(1)} %broadcast_select_fusion.chi_ref, bf16[2048,1024]{1,0:T(8,128)(2,1)S(1)} %get-tuple-element.7.right), custom_call_target="tpu_custom_call" | custom-call | flops 3221225472 | bytes 524288 | tf_op jit(solution)/shard_map/ladder/pallas_call | solution.py:100
  63.9 1.2 collective-permute-start.18
  65.1 1.4 collective-permute-start.20
  66.5 1.9 %collective-permute-start.22 = (bf16[2,64,1024]{2,1,0:T(8,128)(2,1)S(1)}, bf16[2,64,1024]{2,1,0:T(8,128)(2,1)S(1)}, u32[]{:S(2)}, u32[]{:S(2)}) collective-permute-start(bf16[2,64,1024]{2,1,0:T(8,128)(2,1)S(1)} %get-tuple-element.8), channel_id=1, source_target_pairs={{0,12},{1,13},{2,14},{3,15},{4,8},{5,9},{6,10},{7,11},{8,4},{9,5},... | collective-permute-start | bytes 786440 | tf_op jit(solution)/shard_map/ppermute | solution.py:274
  68.4 4.6 %ladder.5.refs_0_ = bf16[2,64,1024]{2,1,0:T(8,128)(2,1)S(1)} custom-call(s32[3]{0:T(128)S(1)} %pad_add_fusion.1.place_ref, f32[2,1024]{1,0:T(2,128)S(1)} %broadcast_select_fusion.chi_ref, bf16[2048,1024]{1,0:T(8,128)(2,1)S(1)} %get-tuple-element.7.right), custom_call_target="tpu_custom_call" | custom-call | flops 3221225472 | bytes 524288 | tf_op jit(solution)/shard_map/ladder/pallas_call | solution.py:100
  73.0 4.6 %collective-permute-done.18.refs_1_ = bf16[2,64,1024]{2,1,0:T(8,128)(2,1)S(1)} collective-permute-done((bf16[2,64,1024]{2,1,0:T(8,128)(2,1)S(1)}, bf16[2,64,1024]{2,1,0:T(8,128)(2,1)S(1)}, u32[]{:S(2)}, u32[]{:S(2)}) %collective-permute-start.18) | collective-permute-done | bytes 262176 | tf_op jit(solution)/shard_map/ppermute | solution.py:274
  77.6 8.8 %collective-permute-done.20.refs_2_ = bf16[2,64,1024]{2,1,0:T(8,128)(2,1)S(1)} collective-permute-done((bf16[2,64,1024]{2,1,0:T(8,128)(2,1)S(1)}, bf16[2,64,1024]{2,1,0:T(8,128)(2,1)S(1)}, u32[]{:S(2)}, u32[]{:S(2)}) %collective-permute-start.20) | collective-permute-done | bytes 262176 | tf_op jit(solution)/shard_map/ppermute | solution.py:274
  86.4 2.0 %select_rows.1 = bf16[256,4096]{1,0:T(8,128)(2,1)} custom-call(bf16[2,256,256]{2,1,0:T(8,128)(2,1)S(1)} %fusion.chosen_ref, bf16[2,64,1024]{2,1,0:T(8,128)(2,1)S(1)} %ladder.5.refs_0_, bf16[2,64,1024]{2,1,0:T(8,128)(2,1)S(1)} %collective-permute-done.18.refs_1_, bf16[2,64,1024]{2,1,0:T(8,128)(2,1)S(1)} %collective-permute-done.20.refs_2_, ...), custom_call_target="tpu_custom_call" | custom-call | flops 536870912 | bytes 4194304 | tf_op jit(solution)/shard_map/select_rows/pallas_call | solution.py:136
  88.5 9.0 %all-to-all-start = ((bf16[32,8,4096]{2,1,0:T(8,128)(2,1)}), bf16[32,8,4096]{2,1,0:T(8,128)(2,1)}, u32[]{:S(2)}, u32[]{:S(2)}) async-start(bf16[32,8,4096]{2,1,0:T(8,128)(2,1)} %bitcast.15), calls=%async_computation | async-start | bytes 4194304 | tf_op jit(solution)/shard_map/all_to_all | solution.py:339
  97.5 0.6 reduce-window.30
  98.1 0.2 slice_reduce_fusion.2
  98.3 0.6 reduce-window.26
  98.9 0.2 slice_reduce_fusion.3
  99.2 0.1 fusion.29
  99.3 0.1 fusion.32
  99.5 0.1 iota_compare_fusion.3
  99.6 0.7 collective-permute-start.17
  100.2 0.7 collective-permute-start.19
  100.9 0.7 collective-permute-start.21
  101.6 0.7 collective-permute-start.23
  102.3 0.1 iota_compare_fusion.4
  102.4 0.8 add_convert_fusion.rows_ref
  103.2 2.3 %total.1 = f32[2,4,64,1024]{3,2,1,0:T(8,128)} custom-call(s32[3]{0:T(128)S(1)} %pad_add_fusion.1.place_ref, f32[2,4,64,1024]{3,2,1,0:T(8,128)S(1)} %copy-done.1, bf16[2,64,1024]{2,1,0:T(8,128)(2,1)S(1)} %collective-permute-done.17.refs_0_, bf16[2,64,1024]{2,1,0:T(8,128)(2,1)S(1)} %collective-permute-done.19.refs_1_, ...), custom_call_target="tpu_custom_call" | custom-call | flops 524288 | bytes 5242880 | tf_op jit(solution)/shard_map/total/pallas_call | solution.py:233
  105.6 42.4 %all-to-all-done = bf16[32,8,4096]{2,1,0:T(8,128)(2,1)} async-done(((bf16[32,8,4096]{2,1,0:T(8,128)(2,1)}), bf16[32,8,4096]{2,1,0:T(8,128)(2,1)}, u32[]{:S(2)}, u32[]{:S(2)}) %all-to-all-start) | async-done | bytes 2097184 | tf_op jit(solution)/shard_map/all_to_all | solution.py:339
  148.0 7.4 %place_rows.1 = (f32[2,256,1024]{2,1,0:T(8,128)}, f32[2,256,1024]{2,1,0:T(8,128)}) custom-call(s32[2,1024]{1,0:T(2,128)} %maps_ref.1, bf16[2,256,256]{2,1,0:T(8,128)(2,1)} %add_convert_fusion.rows_ref, bf16[256,4096]{1,0:T(8,128)(2,1)} %bitcast.16.got, f32[2,256,1024]{2,1,0:T(8,128)} %bitcast.109, f32[2,256,1024]{2,1,0:T(8,128)} %bitcast.110), custom_call_target="tpu_custom_call" | custom-call | flops 2684354560 | bytes 8388608 | tf_op jit(solution)/shard_map/place_rows/pallas_call | solution.py:190
  (54 shorter events, 0.8 us)
Async XLA Ops:
  0.6 0.8 copy-start
  0.6 9.0 %copy-start.2 = (s32[2,8,1024]{2,1,0:T(8,128)S(1)}, s32[2,8,1024]{2,1,0:T(8,128)}, u32[]{:S(2)}) copy-start(s32[2,8,1024]{2,1,0:T(8,128)} %param.10) | copy-start | bytes 196612
  1.4 15.3 %collective-permute-start = (f32[2,1024]{1,0:T(2,128)S(1)}, f32[2,1024]{1,0:T(2,128)S(1)}, u32[]{:S(2)}, u32[]{:S(2)}) collective-permute-start(f32[2,1024]{1,0:T(2,128)S(1)} %bitcast.108), channel_id=1, source_target_pairs={{0,16},{1,17},{2,18},{3,19},{4,20},{5,21},{6,22},{7,23},{8,24},{9,... | collective-permute-start | bytes 24584 | tf_op jit(solution)/shard_map/ppermute | solution.py:274
  3.7 9.5 %collective-permute-start.1 = (bf16[2,64,1024]{2,1,0:T(8,128)(2,1)S(1)}, bf16[2,64,1024]{2,1,0:T(8,128)(2,1)S(1)}, u32[]{:S(2)}, u32[]{:S(2)}) collective-permute-start(bf16[2,64,1024]{2,1,0:T(8,128)(2,1)S(1)} %get-tuple-element.14), channel_id=1, source_target_pairs={{0,0},{1,1},{2,16},{3,17},{4,4},{5,5},{6,20},{7,21},{8,8},{9,9},{1... | collective-permute-start | bytes 786440 | tf_op jit(solution)/shard_map/ppermute | solution.py:274
  4.3 14.9 %collective-permute-start.5 = (bf16[2,64,1024]{2,1,0:T(8,128)(2,1)S(1)}, bf16[2,64,1024]{2,1,0:T(8,128)(2,1)S(1)}, u32[]{:S(2)}, u32[]{:S(2)}) collective-permute-start(bf16[2,64,1024]{2,1,0:T(8,128)(2,1)S(1)} %get-tuple-element.13), channel_id=1, source_target_pairs={{0,4},{1,5},{2,20},{3,21},{4,0},{5,1},{6,16},{7,17},{8,12},{9,13},... | collective-permute-start | bytes 786440 | tf_op jit(solution)/shard_map/ppermute | solution.py:274
  7.0 12.3 %collective-permute-start.9 = (bf16[2,64,1024]{2,1,0:T(8,128)(2,1)S(1)}, bf16[2,64,1024]{2,1,0:T(8,128)(2,1)S(1)}, u32[]{:S(2)}, u32[]{:S(2)}) collective-permute-start(bf16[2,64,1024]{2,1,0:T(8,128)(2,1)S(1)} %get-tuple-element.12), channel_id=1, source_target_pairs={{0,8},{1,9},{2,24},{3,25},{4,12},{5,13},{6,28},{7,29},{8,0},{9,1},... | collective-permute-start | bytes 786440 | tf_op jit(solution)/shard_map/ppermute | solution.py:274
  9.6 16.2 %collective-permute-start.13 = (bf16[2,64,1024]{2,1,0:T(8,128)(2,1)S(1)}, bf16[2,64,1024]{2,1,0:T(8,128)(2,1)S(1)}, u32[]{:S(2)}, u32[]{:S(2)}) collective-permute-start(bf16[2,64,1024]{2,1,0:T(8,128)(2,1)S(1)} %get-tuple-element.11), channel_id=1, source_target_pairs={{0,12},{1,13},{2,28},{3,29},{4,8},{5,9},{6,24},{7,25},{8,4},{9,5},... | collective-permute-start | bytes 786440 | tf_op jit(solution)/shard_map/ppermute | solution.py:274
  13.2 19.2 %collective-permute-start.2 = (bf16[2,64,1024]{2,1,0:T(8,128)(2,1)S(1)}, bf16[2,64,1024]{2,1,0:T(8,128)(2,1)S(1)}, u32[]{:S(2)}, u32[]{:S(2)}) collective-permute-start(bf16[2,64,1024]{2,1,0:T(8,128)(2,1)S(1)} %collective-permute-done.1.refs_0_), channel_id=1, source_target_pairs={{0,16},{1,17},{2,18},{3,19},{4,20},{5,21},{6,22},{7,23},{8,24},{9,... | collective-permute-start | bytes 786440 | tf_op jit(solution)/shard_map/ppermute | solution.py:274
  16.7 16.2 %collective-permute-start.3 = (bf16[2,64,1024]{2,1,0:T(8,128)(2,1)S(1)}, bf16[2,64,1024]{2,1,0:T(8,128)(2,1)S(1)}, u32[]{:S(2)}, u32[]{:S(2)}) collective-permute-start(bf16[2,64,1024]{2,1,0:T(8,128)(2,1)S(1)} %collective-permute-done.1.refs_0_), channel_id=1, source_target_pairs={{0,1},{1,0},{2,3},{3,2},{4,5},{5,4},{6,7},{7,6},{8,9},{9,8},{10,11... | collective-permute-start | bytes 786440 | tf_op jit(solution)/shard_map/ppermute | solution.py:274
  19.2 15.3 %collective-permute-start.6 = (bf16[2,64,1024]{2,1,0:T(8,128)(2,1)S(1)}, bf16[2,64,1024]{2,1,0:T(8,128)(2,1)S(1)}, u32[]{:S(2)}, u32[]{:S(2)}) collective-permute-start(bf16[2,64,1024]{2,1,0:T(8,128)(2,1)S(1)} %collective-permute-done.5.refs_4_), channel_id=1, source_target_pairs={{0,16},{1,17},{2,18},{3,19},{4,20},{5,21},{6,22},{7,23},{8,24},{9,... | collective-permute-start | bytes 786440 | tf_op jit(solution)/shard_map/ppermute | solution.py:274
  19.3 15.3 %collective-permute-start.7 = (bf16[2,64,1024]{2,1,0:T(8,128)(2,1)S(1)}, bf16[2,64,1024]{2,1,0:T(8,128)(2,1)S(1)}, u32[]{:S(2)}, u32[]{:S(2)}) collective-permute-start(bf16[2,64,1024]{2,1,0:T(8,128)(2,1)S(1)} %collective-permute-done.5.refs_4_), channel_id=1, source_target_pairs={{0,1},{1,0},{2,3},{3,2},{4,5},{5,4},{6,7},{7,6},{8,9},{9,8},{10,11... | collective-permute-start | bytes 786440 | tf_op jit(solution)/shard_map/ppermute | solution.py:274
  25.8 11.5 %collective-permute-start.10 = (bf16[2,64,1024]{2,1,0:T(8,128)(2,1)S(1)}, bf16[2,64,1024]{2,1,0:T(8,128)(2,1)S(1)}, u32[]{:S(2)}, u32[]{:S(2)}) collective-permute-start(bf16[2,64,1024]{2,1,0:T(8,128)(2,1)S(1)} %collective-permute-done.9.refs_8_), channel_id=1, source_target_pairs={{0,16},{1,17},{2,18},{3,19},{4,20},{5,21},{6,22},{7,23},{8,24},{9,... | collective-permute-start | bytes 786440 | tf_op jit(solution)/shard_map/ppermute | solution.py:274
  32.4 9.2 %collective-permute-start.11 = (bf16[2,64,1024]{2,1,0:T(8,128)(2,1)S(1)}, bf16[2,64,1024]{2,1,0:T(8,128)(2,1)S(1)}, u32[]{:S(2)}, u32[]{:S(2)}) collective-permute-start(bf16[2,64,1024]{2,1,0:T(8,128)(2,1)S(1)} %collective-permute-done.9.refs_8_), channel_id=1, source_target_pairs={{0,1},{1,0},{2,3},{3,2},{4,5},{5,4},{6,7},{7,6},{8,9},{9,8},{10,11... | collective-permute-start | bytes 786440 | tf_op jit(solution)/shard_map/ppermute | solution.py:274
  32.9 14.3 %collective-permute-start.15 = (bf16[2,64,1024]{2,1,0:T(8,128)(2,1)S(1)}, bf16[2,64,1024]{2,1,0:T(8,128)(2,1)S(1)}, u32[]{:S(2)}, u32[]{:S(2)}) collective-permute-start(bf16[2,64,1024]{2,1,0:T(8,128)(2,1)S(1)} %collective-permute-done.13.refs_12_), channel_id=1, source_target_pairs={{0,1},{1,0},{2,3},{3,2},{4,5},{5,4},{6,7},{7,6},{8,9},{9,8},{10,11... | collective-permute-start | bytes 786440 | tf_op jit(solution)/shard_map/ppermute | solution.py:274
  34.6 13.1 %collective-permute-start.14 = (bf16[2,64,1024]{2,1,0:T(8,128)(2,1)S(1)}, bf16[2,64,1024]{2,1,0:T(8,128)(2,1)}, u32[]{:S(2)}, u32[]{:S(2)}) collective-permute-start(bf16[2,64,1024]{2,1,0:T(8,128)(2,1)S(1)} %collective-permute-done.13.refs_12_), channel_id=1, source_target_pairs={{0,16},{1,17},{2,18},{3,19},{4,20},{5,21},{6,22},{7,23},{8,24},{9,... | collective-permute-start | bytes 786440 | tf_op jit(solution)/shard_map/ppermute | solution.py:274
  34.7 13.1 %collective-permute-start.4 = (bf16[2,64,1024]{2,1,0:T(8,128)(2,1)S(1)}, bf16[2,64,1024]{2,1,0:T(8,128)(2,1)}, u32[]{:S(2)}, u32[]{:S(2)}) collective-permute-start(bf16[2,64,1024]{2,1,0:T(8,128)(2,1)S(1)} %collective-permute-done.3.refs_2_), channel_id=1, source_target_pairs={{0,16},{1,17},{2,18},{3,19},{4,20},{5,21},{6,22},{7,23},{8,24},{9,... | collective-permute-start | bytes 786440 | tf_op jit(solution)/shard_map/ppermute | solution.py:274
  37.3 10.4 %collective-permute-start.8 = (bf16[2,64,1024]{2,1,0:T(8,128)(2,1)S(1)}, bf16[2,64,1024]{2,1,0:T(8,128)(2,1)}, u32[]{:S(2)}, u32[]{:S(2)}) collective-permute-start(bf16[2,64,1024]{2,1,0:T(8,128)(2,1)S(1)} %collective-permute-done.7.refs_6_), channel_id=1, source_target_pairs={{0,16},{1,17},{2,18},{3,19},{4,20},{5,21},{6,22},{7,23},{8,24},{9,... | collective-permute-start | bytes 786440 | tf_op jit(solution)/shard_map/ppermute | solution.py:274
  41.6 6.2 %collective-permute-start.12 = (bf16[2,64,1024]{2,1,0:T(8,128)(2,1)S(1)}, bf16[2,64,1024]{2,1,0:T(8,128)(2,1)}, u32[]{:S(2)}, u32[]{:S(2)}) collective-permute-start(bf16[2,64,1024]{2,1,0:T(8,128)(2,1)S(1)} %collective-permute-done.11.refs_10_), channel_id=1, source_target_pairs={{0,16},{1,17},{2,18},{3,19},{4,20},{5,21},{6,22},{7,23},{8,24},{9,... | collective-permute-start | bytes 786440 | tf_op jit(solution)/shard_map/ppermute | solution.py:274
  47.2 1.7 %collective-permute-start.16 = (bf16[2,64,1024]{2,1,0:T(8,128)(2,1)S(1)}, bf16[2,64,1024]{2,1,0:T(8,128)(2,1)}, u32[]{:S(2)}, u32[]{:S(2)}) collective-permute-start(bf16[2,64,1024]{2,1,0:T(8,128)(2,1)S(1)} %collective-permute-done.15.refs_14_), channel_id=1, source_target_pairs={{0,16},{1,17},{2,18},{3,19},{4,20},{5,21},{6,22},{7,23},{8,24},{9,... | collective-permute-start | bytes 786440 | tf_op jit(solution)/shard_map/ppermute | solution.py:274
  63.9 13.7 %collective-permute-start.18 = (bf16[2,64,1024]{2,1,0:T(8,128)(2,1)S(1)}, bf16[2,64,1024]{2,1,0:T(8,128)(2,1)S(1)}, u32[]{:S(2)}, u32[]{:S(2)}) collective-permute-start(bf16[2,64,1024]{2,1,0:T(8,128)(2,1)S(1)} %ladder.6), channel_id=1, source_target_pairs={{0,4},{1,5},{2,6},{3,7},{4,0},{5,1},{6,2},{7,3},{8,12},{9,13},{10,... | collective-permute-start | bytes 786440 | tf_op jit(solution)/shard_map/ppermute | solution.py:274
  65.1 21.3 %collective-permute-start.20 = (bf16[2,64,1024]{2,1,0:T(8,128)(2,1)S(1)}, bf16[2,64,1024]{2,1,0:T(8,128)(2,1)S(1)}, u32[]{:S(2)}, u32[]{:S(2)}) collective-permute-start(bf16[2,64,1024]{2,1,0:T(8,128)(2,1)S(1)} %ladder.7), channel_id=1, source_target_pairs={{0,8},{1,9},{2,10},{3,11},{4,12},{5,13},{6,14},{7,15},{8,0},{9,1},... | collective-permute-start | bytes 786440 | tf_op jit(solution)/shard_map/ppermute | solution.py:274
  66.5 20.0 %collective-permute-start.22 = (bf16[2,64,1024]{2,1,0:T(8,128)(2,1)S(1)}, bf16[2,64,1024]{2,1,0:T(8,128)(2,1)S(1)}, u32[]{:S(2)}, u32[]{:S(2)}) collective-permute-start(bf16[2,64,1024]{2,1,0:T(8,128)(2,1)S(1)} %get-tuple-element.8), channel_id=1, source_target_pairs={{0,12},{1,13},{2,14},{3,15},{4,8},{5,9},{6,10},{7,11},{8,4},{9,5},... | collective-permute-start | bytes 786440 | tf_op jit(solution)/shard_map/ppermute | solution.py:274
  88.5 14.7 %copy-start.1 = (f32[2,4,64,1024]{3,2,1,0:T(8,128)S(1)}, f32[2,4,64,1024]{3,2,1,0:T(8,128)}, u32[]{:S(2)}) copy-start(f32[2,4,64,1024]{3,2,1,0:T(8,128)} %vertex.1) | copy-start | bytes 6291460
  88.5 59.5 %all-to-all-start = ((bf16[32,8,4096]{2,1,0:T(8,128)(2,1)}), bf16[32,8,4096]{2,1,0:T(8,128)(2,1)}, u32[]{:S(2)}, u32[]{:S(2)}) async-start(bf16[32,8,4096]{2,1,0:T(8,128)(2,1)} %bitcast.15), calls=%async_computation | async-start | bytes 4194304 | tf_op jit(solution)/shard_map/all_to_all | solution.py:339
  99.6 3.6 %collective-permute-start.17 = (bf16[2,64,1024]{2,1,0:T(8,128)(2,1)S(1)}, bf16[2,64,1024]{2,1,0:T(8,128)(2,1)S(1)}, u32[]{:S(2)}, u32[]{:S(2)}) collective-permute-start(bf16[2,64,1024]{2,1,0:T(8,128)(2,1)S(1)} %ladder.5.refs_0_), channel_id=1, source_target_pairs={{0,0},{1,1},{2,16},{3,17},{4,4},{5,5},{6,20},{7,21},{8,8},{9,9},{1... | collective-permute-start | bytes 786440 | tf_op jit(solution)/shard_map/ppermute | solution.py:274
  100.2 2.9 %collective-permute-start.19 = (bf16[2,64,1024]{2,1,0:T(8,128)(2,1)S(1)}, bf16[2,64,1024]{2,1,0:T(8,128)(2,1)S(1)}, u32[]{:S(2)}, u32[]{:S(2)}) collective-permute-start(bf16[2,64,1024]{2,1,0:T(8,128)(2,1)S(1)} %collective-permute-done.18.refs_1_), channel_id=1, source_target_pairs={{0,0},{1,1},{2,16},{3,17},{4,4},{5,5},{6,20},{7,21},{8,8},{9,9},{1... | collective-permute-start | bytes 786440 | tf_op jit(solution)/shard_map/ppermute | solution.py:274
  100.9 2.2 %collective-permute-start.21 = (bf16[2,64,1024]{2,1,0:T(8,128)(2,1)S(1)}, bf16[2,64,1024]{2,1,0:T(8,128)(2,1)S(1)}, u32[]{:S(2)}, u32[]{:S(2)}) collective-permute-start(bf16[2,64,1024]{2,1,0:T(8,128)(2,1)S(1)} %collective-permute-done.20.refs_2_), channel_id=1, source_target_pairs={{0,0},{1,1},{2,16},{3,17},{4,4},{5,5},{6,20},{7,21},{8,8},{9,9},{1... | collective-permute-start | bytes 786440 | tf_op jit(solution)/shard_map/ppermute | solution.py:274
  101.6 1.6 %collective-permute-start.23 = (bf16[2,64,1024]{2,1,0:T(8,128)(2,1)S(1)}, bf16[2,64,1024]{2,1,0:T(8,128)(2,1)S(1)}, u32[]{:S(2)}, u32[]{:S(2)}) collective-permute-start(bf16[2,64,1024]{2,1,0:T(8,128)(2,1)S(1)} %collective-permute-done.22.refs_3_), channel_id=1, source_target_pairs={{0,0},{1,1},{2,16},{3,17},{4,4},{5,5},{6,20},{7,21},{8,8},{9,9},{1... | collective-permute-start | bytes 786440 | tf_op jit(solution)/shard_map/ppermute | solution.py:274

commit v3 on v2

--- a/solution.py
+++ b/solution.py
@@ -146,39 +146,45 @@
     )(chosen, *returned)
 
 
-def place_kernel(maps_ref, rows_ref, got, base_a, base_b, out_a, out_b, *scratch):
-    columns, base, moved, in_sems, out_sems = scratch
+def place_kernel(maps_ref, rows_ref, received, base_a, base_b, out_a, out_b, *scratch):
+    columns, got, base, moved, got_sems, in_sems, out_sems = scratch
     depth = columns.shape[1]
     bases, outs = (base_a, base_b), (out_a, out_b)
-    arriving, leaving = {}, []
+    landing, arriving, leaving = {}, {}, []
     for channel in range(2):
         for part in range(2):
-            copy = pltpu.make_async_copy(
+            span = pl.ds((channel * 2 + part) * depth, depth)
+            landing[channel, part] = pltpu.make_async_copy(
+                received.at[:, span], got.at[channel, part], got_sems.at[channel, part]
+            )
+            arriving[channel, part] = pltpu.make_async_copy(
                 bases[channel].at[part], base.at[channel, part], in_sems.at[channel, part]
             )
-            copy.start()
-            arriving[channel, part] = copy
+    turns = [(channel, part) for channel in range(2) for part in range(2)]
+    for turn in turns[:2]:
+        landing[turn].start()
+        arriving[turn].start()
     wide = lax.broadcasted_iota(jnp.int32, (depth, depth), 0)
     for channel in range(2):
         hit = wide == maps_ref[channel : channel + 1, :]
         columns[channel] = jnp.where(hit, 1.0, 0.0).astype(jnp.bfloat16)
-    for channel in range(2):
-        for part in range(2):
-            start = (channel * 2 + part) * depth
-            picked = jnp.dot(
-                rows_ref[channel],
-                got[:, start : start + depth],
-                preferred_element_type=jnp.float32,
-            ).astype(jnp.bfloat16)
-            arriving[channel, part].wait()
-            moved[channel, part] = base[channel, part] + jnp.dot(
-                picked, columns[channel], preferred_element_type=jnp.float32
-            )
-            copy = pltpu.make_async_copy(
-                moved.at[channel, part], outs[channel].at[part], out_sems.at[channel, part]
-            )
-            copy.start()
-            leaving.append(copy)
+    for number, (channel, part) in enumerate(turns):
+        landing[channel, part].wait()
+        if number + 2 < len(turns):
+            landing[turns[number + 2]].start()
+            arriving[turns[number + 2]].start()
+        picked = jnp.dot(
+            rows_ref[channel], got[channel, part], preferred_element_type=jnp.float32
+        ).astype(jnp.bfloat16)
+        arriving[channel, part].wait()
+        moved[channel, part] = base[channel, part] + jnp.dot(
+            picked, columns[channel], preferred_element_type=jnp.float32
+        )
+        copy = pltpu.make_async_copy(
+            moved.at[channel, part], outs[channel].at[part], out_sems.at[channel, part]
+        )
+        copy.start()
+        leaving.append(copy)
     for copy in leaving:
         copy.wait()
 
@@ -190,12 +196,14 @@
     return pl.pallas_call(
         place_kernel,
         out_shape=[jax.ShapeDtypeStruct((2, count, depth), jnp.float32)] * 2,
-        in_specs=[vmem, vmem, vmem, hbm, hbm],
+        in_specs=[vmem, vmem, hbm, hbm, hbm],
         out_specs=[hbm, hbm],
         scratch_shapes=[
             pltpu.VMEM((2, depth, depth), jnp.bfloat16),
+            pltpu.VMEM((2, 2, slots, depth), jnp.bfloat16),
             pltpu.VMEM((2, 2, count, depth), jnp.float32),
             pltpu.VMEM((2, 2, count, depth), jnp.float32),
+            pltpu.SemaphoreType.DMA((2, 2)),
             pltpu.SemaphoreType.DMA((2, 2)),
             pltpu.SemaphoreType.DMA((2, 2)),
         ],
@@ -273,13 +281,18 @@
     def move(value, target):
         return lax.ppermute(value, ("pb", "ka"), [(i, target(i)) for i in range(dev_count)])
 
-    def piece_of(index):
-        piece = lax.dynamic_index_in_dim(vertex_ladder, index, 1, keepdims=False)
+    def piece_of(whole, index):
+        piece = lax.dynamic_index_in_dim(whole, index, 1, keepdims=False)
         return piece.astype(jnp.bfloat16)
 
     held = {}
+    first = [0, q_local - 1]
+    cast = [piece_of(vertex_ladder, group ^ d) for d in first]
+    *cast, whole = lax.optimization_barrier((*cast, vertex_ladder))
+    cast = dict(zip(first, cast))
     for d in range(q_local):
-        held[d, 0, 0] = move(piece_of(group ^ d), lambda i, d=d: twin_of(i) ^ (d * plane))
+        piece = cast[d] if d in cast else piece_of(whole, group ^ d)
+        held[d, 0, 0] = move(piece, lambda i, d=d: twin_of(i) ^ (d * plane))
     bits = [1 << b for b in range(low_count.bit_length() - 1)]
     for d in range(q_local):
         have = [0]
@@ -307,9 +320,19 @@
     def device_of(global_rows):
         return global_rows // col_count // q_local * ka_count + global_rows % col_count // row_count
 
+    def ranks(flags, axis):
+        count = jnp.arange(flags.shape[axis], dtype=jnp.int32)
+        before = (count[:, None] <= count[None, :]).astype(jnp.bfloat16)
+        low_flags = flags.astype(jnp.bfloat16)
+        if axis == 1:
+            sums = jnp.dot(low_flags, before, preferred_element_type=jnp.float32)
+        else:
+            sums = jnp.dot(before.T, low_flags, preferred_element_type=jnp.float32)
+        return sums.astype(jnp.int32)
+
     def chosen_of(by_device):
         mine = (device_of(by_device) == my_twin).astype(jnp.int32)
-        rank = jnp.cumsum(mine, 1) - 1
+        rank = ranks(mine, 1) - 1
         source_q = by_device // col_count % q_local
         source_place = (source_q ^ group) * row_count + by_device % col_count % row_count
         slot_ids = jnp.arange(per_peer, dtype=jnp.int32)
@@ -323,7 +346,7 @@
         onehot = (source_dev[:, None] == jnp.arange(dev_count, dtype=jnp.int32)[None, :]).astype(
             jnp.int32
         )
-        slot_index = jnp.sum((jnp.cumsum(onehot, 0) - onehot) * onehot, 1)
+        slot_index = jnp.sum((ranks(onehot, 0) - onehot) * onehot, 1)
         return twin_of(source_dev), slot_index
 
     tables = [
@@ -362,7 +385,7 @@
 
 
 def parts_of(q_local):
-    return [(d,) for d in range(q_local - 1, -1, -1)]
+    return [(q_local - 1,), *((d,) for d in range(1, q_local - 1)), (0,)]
 
 
 def solution(mesh):

time: 156 us -> 157 us (level)
  other arithmetic: 5.81 us -> 2.77 us
  starting transfers between devices: 41.9 us -> 44.1 us
  waiting for transfers between devices: 71.2 us -> 72.8 us
    another operation x8 -> x0, other arithmetic: 2.51 us -> none
    ppermute x24, starting transfers between devices: 33 us -> 35.1 us  [move(): lax.ppermute(value, ('pb', 'ka'), [(i, target(i)) for i in range(dev_coun...]
  transfers between devices with their start and end apart: 25 -> 25, of which waited for: 7 -> 7; matrix products, arithmetic and copies ran while one was open for 6% -> 4% of each run, Pallas kernels for 4% -> 4%
where the time goes in v3:
time: 157 us; the launch traced here: 156 us
  waiting for transfers between devices  72.8 us (46%)
  starting transfers between devices  44.1 us (28%)
  Pallas kernels  31 us (20%)
  local copies, waits for them, and re-layouts  3.91 us (2%)
  other arithmetic  2.77 us (2%)
    all_to_all x1, waiting for transfers between devices, per_device(): lax.all_to_all(send.reshape(dev_count, per_peer, 4 * col_count), ('pb', '...  44 us
    ppermute x24, starting transfers between devices, move(): lax.ppermute(value, ('pb', 'ka'), [(i, target(i)) for i in range(dev_coun...  35.1 us
    ppermute x24, waiting for transfers between devices, move(): lax.ppermute(value, ('pb', 'ka'), [(i, target(i)) for i in range(dev_coun...  28.8 us
    pallas_call x4, Pallas kernels, ladder(): pl.pallas_call(functools.partial(first_kernel if first else next_kernel,...  19.6 us
    all_to_all x1, starting transfers between devices, per_device(): lax.all_to_all(send.reshape(dev_count, per_peer, 4 * col_count), ('pb', '...  8.93 us
    pallas_call x1, Pallas kernels, place_rows(): pl.pallas_call(place_kernel, out_shape=[jax.ShapeDtypeStruct((2, count, d...  7.23 us
  transfers between devices with their start and end apart: 25, of which 7 were waited for; matrix products, arithmetic and copies ran while one was open for 4% of the time, Pallas kernels for 4%

profile of v3, /device:TPU:0, one launch (start us, length us, event | category | flops | bytes accessed | tf_op | source)
XLA Modules:
  0.0 156.3 jit_solution(12740798310795625032)
XLA Ops:
  0.6 0.0 copy-start
  0.7 0.7 copy-done
  1.4 0.6 collective-permute-start
  2.0 1.3 fusion.12
  3.2 0.7 collective-permute-start.1
  3.9 1.3 fusion.10
  5.2 2.7 %collective-permute-start.5 = (bf16[2,64,1024]{2,1,0:T(8,128)(2,1)S(1)}, bf16[2,64,1024]{2,1,0:T(8,128)(2,1)S(1)}, u32[]{:S(2)}, u32[]{:S(2)}) collective-permute-start(bf16[2,64,1024]{2,1,0:T(8,128)(2,1)S(1)} %get-tuple-element.20), channel_id=1, source_target_pairs={{0,4},{1,5},{2,20},{3,21},{4,0},{5,1},{6,16},{7,17},{8,12},{9,13},... | collective-permute-start | bytes 786440 | tf_op jit(solution)/shard_map/ppermute | solution.py:282
  7.9 2.6 %collective-permute-start.9 = (bf16[2,64,1024]{2,1,0:T(8,128)(2,1)S(1)}, bf16[2,64,1024]{2,1,0:T(8,128)(2,1)S(1)}, u32[]{:S(2)}, u32[]{:S(2)}) collective-permute-start(bf16[2,64,1024]{2,1,0:T(8,128)(2,1)S(1)} %get-tuple-element.19), channel_id=1, source_target_pairs={{0,8},{1,9},{2,24},{3,25},{4,12},{5,13},{6,28},{7,29},{8,0},{9,1},... | collective-permute-start | bytes 786440 | tf_op jit(solution)/shard_map/ppermute | solution.py:282
  10.5 0.0 collective-permute-start.13
  10.5 0.1 reshape_squeeze.7
  10.6 0.1 reshape.682
  10.7 0.1 reshape_squeeze.6
  10.8 0.1 reshape.681
  10.9 0.1 fusion.18
  11.0 0.1 fusion.31
  11.2 0.2 fusion
  11.3 0.6 multiply_reduce_fusion
  12.0 0.1 stack.32
  12.1 3.5 %collective-permute-start.2 = (bf16[2,64,1024]{2,1,0:T(8,128)(2,1)S(1)}, bf16[2,64,1024]{2,1,0:T(8,128)(2,1)S(1)}, u32[]{:S(2)}, u32[]{:S(2)}) collective-permute-start(bf16[2,64,1024]{2,1,0:T(8,128)(2,1)S(1)} %collective-permute-done.1.refs_0_), channel_id=1, source_target_pairs={{0,16},{1,17},{2,18},{3,19},{4,20},{5,21},{6,22},{7,23},{8,24},{9,... | collective-permute-start | bytes 786440 | tf_op jit(solution)/shard_map/ppermute | solution.py:282
  15.6 0.0 collective-permute-done
  15.6 1.7 %collective-permute-start.3 = (bf16[2,64,1024]{2,1,0:T(8,128)(2,1)S(1)}, bf16[2,64,1024]{2,1,0:T(8,128)(2,1)S(1)}, u32[]{:S(2)}, u32[]{:S(2)}) collective-permute-start(bf16[2,64,1024]{2,1,0:T(8,128)(2,1)S(1)} %collective-permute-done.1.refs_0_), channel_id=1, source_target_pairs={{0,1},{1,0},{2,3},{3,2},{4,5},{5,4},{6,7},{7,6},{8,9},{9,8},{10,11... | collective-permute-start | bytes 786440 | tf_op jit(solution)/shard_map/ppermute | solution.py:282
  17.4 0.2 fusion.1
  17.5 0.6 multiply_reduce_fusion.1
  18.2 0.1 stack.31
  18.2 1.3 collective-permute-start.6
  19.6 1.5 collective-permute-start.7
  21.1 5.6 %collective-permute-done.13.refs_12_ = bf16[2,64,1024]{2,1,0:T(8,128)(2,1)S(1)} collective-permute-done((bf16[2,64,1024]{2,1,0:T(8,128)(2,1)S(1)}, bf16[2,64,1024]{2,1,0:T(8,128)(2,1)S(1)}, u32[]{:S(2)}, u32[]{:S(2)}) %collective-permute-start.13) | collective-permute-done | bytes 262176 | tf_op jit(solution)/shard_map/ppermute | solution.py:282
  26.6 6.6 %collective-permute-start.10 = (bf16[2,64,1024]{2,1,0:T(8,128)(2,1)S(1)}, bf16[2,64,1024]{2,1,0:T(8,128)(2,1)S(1)}, u32[]{:S(2)}, u32[]{:S(2)}) collective-permute-start(bf16[2,64,1024]{2,1,0:T(8,128)(2,1)S(1)} %collective-permute-done.9.refs_8_), channel_id=1, source_target_pairs={{0,16},{1,17},{2,18},{3,19},{4,20},{5,21},{6,22},{7,23},{8,24},{9,... | collective-permute-start | bytes 786440 | tf_op jit(solution)/shard_map/ppermute | solution.py:282
  33.3 0.5 collective-permute-start.11
  33.8 1.5 collective-permute-start.15
  35.3 0.1 fusion.8.chosen_ref
  35.5 0.1 collective-permute-start.14
  35.6 2.6 %collective-permute-start.4 = (bf16[2,64,1024]{2,1,0:T(8,128)(2,1)S(1)}, bf16[2,64,1024]{2,1,0:T(8,128)(2,1)}, u32[]{:S(2)}, u32[]{:S(2)}) collective-permute-start(bf16[2,64,1024]{2,1,0:T(8,128)(2,1)S(1)} %collective-permute-done.3.refs_2_), channel_id=1, source_target_pairs={{0,16},{1,17},{2,18},{3,19},{4,20},{5,21},{6,22},{7,23},{8,24},{9,... | collective-permute-start | bytes 786440 | tf_op jit(solution)/shard_map/ppermute | solution.py:282
  38.2 0.0 collective-permute-start.8
  38.2 4.3 %collective-permute-done.11.refs_10_ = bf16[2,64,1024]{2,1,0:T(8,128)(2,1)S(1)} collective-permute-done((bf16[2,64,1024]{2,1,0:T(8,128)(2,1)S(1)}, bf16[2,64,1024]{2,1,0:T(8,128)(2,1)S(1)}, u32[]{:S(2)}, u32[]{:S(2)}) %collective-permute-start.11) | collective-permute-done | bytes 262176 | tf_op jit(solution)/shard_map/ppermute | solution.py:282
  42.5 1.3 collective-permute-start.12
  43.8 4.3 %collective-permute-done.15.refs_14_ = bf16[2,64,1024]{2,1,0:T(8,128)(2,1)S(1)} collective-permute-done((bf16[2,64,1024]{2,1,0:T(8,128)(2,1)S(1)}, bf16[2,64,1024]{2,1,0:T(8,128)(2,1)S(1)}, u32[]{:S(2)}, u32[]{:S(2)}) %collective-permute-start.15) | collective-permute-done | bytes 262176 | tf_op jit(solution)/shard_map/ppermute | solution.py:282
  48.1 0.4 collective-permute-start.16
  48.5 0.1 pad_add_fusion.1.place_ref
  48.6 1.2 collective-permute-done.16.refs_15_
  49.8 5.6 %ladder.4 = (bf16[2,64,1024]{2,1,0:T(8,128)(2,1)S(1)}, bf16[2048,1024]{1,0:T(8,128)(2,1)S(1)}) custom-call(s32[3]{0:T(128)S(1)} %pad_add_fusion.1.place_ref, f32[2,1024]{1,0:T(2,128)S(1)} %broadcast_select_fusion.chi_ref, bf16[2,64,1024]{2,1,0:T(8,128)(2,1)S(1)} %collective-permute-done.1.refs_0_, bf16[2,64,1024]{2,1,0:T(8,128)(2,1)S(1)} %collective-permute-done.2.refs_1_, ...), custom_call_target="tpu_custom_call" | custom-call | flops 3221225472 | bytes 4718592 | tf_op jit(solution)/shard_map/ladder/pallas_call | solution.py:100
  55.4 4.6 %ladder.6 = bf16[2,64,1024]{2,1,0:T(8,128)(2,1)S(1)} custom-call(s32[3]{0:T(128)S(1)} %pad_add_fusion.1.place_ref, f32[2,1024]{1,0:T(2,128)S(1)} %broadcast_select_fusion.chi_ref, bf16[2048,1024]{1,0:T(8,128)(2,1)S(1)} %get-tuple-element.13.right), custom_call_target="tpu_custom_call" | custom-call | flops 3221225472 | bytes 524288 | tf_op jit(solution)/shard_map/ladder/pallas_call | solution.py:100
  60.0 4.8 %ladder.7 = bf16[2,64,1024]{2,1,0:T(8,128)(2,1)S(1)} custom-call(s32[3]{0:T(128)S(1)} %pad_add_fusion.1.place_ref, f32[2,1024]{1,0:T(2,128)S(1)} %broadcast_select_fusion.chi_ref, bf16[2048,1024]{1,0:T(8,128)(2,1)S(1)} %get-tuple-element.13.right), custom_call_target="tpu_custom_call" | custom-call | flops 3221225472 | bytes 524288 | tf_op jit(solution)/shard_map/ladder/pallas_call | solution.py:100
  64.8 1.2 collective-permute-start.18
  66.0 1.4 collective-permute-start.20
  67.4 1.9 %collective-permute-start.22 = (bf16[2,64,1024]{2,1,0:T(8,128)(2,1)S(1)}, bf16[2,64,1024]{2,1,0:T(8,128)(2,1)S(1)}, u32[]{:S(2)}, u32[]{:S(2)}) collective-permute-start(bf16[2,64,1024]{2,1,0:T(8,128)(2,1)S(1)} %get-tuple-element.14), channel_id=1, source_target_pairs={{0,12},{1,13},{2,14},{3,15},{4,8},{5,9},{6,10},{7,11},{8,4},{9,5},... | collective-permute-start | bytes 786440 | tf_op jit(solution)/shard_map/ppermute | solution.py:282
  69.3 4.6 %ladder.5.refs_0_ = bf16[2,64,1024]{2,1,0:T(8,128)(2,1)S(1)} custom-call(s32[3]{0:T(128)S(1)} %pad_add_fusion.1.place_ref, f32[2,1024]{1,0:T(2,128)S(1)} %broadcast_select_fusion.chi_ref, bf16[2048,1024]{1,0:T(8,128)(2,1)S(1)} %get-tuple-element.13.right), custom_call_target="tpu_custom_call" | custom-call | flops 3221225472 | bytes 524288 | tf_op jit(solution)/shard_map/ladder/pallas_call | solution.py:100
  73.9 4.6 %collective-permute-done.18.refs_1_ = bf16[2,64,1024]{2,1,0:T(8,128)(2,1)S(1)} collective-permute-done((bf16[2,64,1024]{2,1,0:T(8,128)(2,1)S(1)}, bf16[2,64,1024]{2,1,0:T(8,128)(2,1)S(1)}, u32[]{:S(2)}, u32[]{:S(2)}) %collective-permute-start.18) | collective-permute-done | bytes 262176 | tf_op jit(solution)/shard_map/ppermute | solution.py:282
  78.5 8.8 %collective-permute-done.20.refs_2_ = bf16[2,64,1024]{2,1,0:T(8,128)(2,1)S(1)} collective-permute-done((bf16[2,64,1024]{2,1,0:T(8,128)(2,1)S(1)}, bf16[2,64,1024]{2,1,0:T(8,128)(2,1)S(1)}, u32[]{:S(2)}, u32[]{:S(2)}) %collective-permute-start.20) | collective-permute-done | bytes 262176 | tf_op jit(solution)/shard_map/ppermute | solution.py:282
  87.4 2.0 %select_rows.1 = bf16[256,4096]{1,0:T(8,128)(2,1)} custom-call(bf16[2,256,256]{2,1,0:T(8,128)(2,1)S(1)} %fusion.8.chosen_ref, bf16[2,64,1024]{2,1,0:T(8,128)(2,1)S(1)} %ladder.5.refs_0_, bf16[2,64,1024]{2,1,0:T(8,128)(2,1)S(1)} %collective-permute-done.18.refs_1_, bf16[2,64,1024]{2,1,0:T(8,128)(2,1)S(1)} %collective-permute-done.20.refs_2_, ...), custom_call_target="tpu_custom_call" | custom-call | flops 536870912 | bytes 4194304 | tf_op jit(solution)/shard_map/select_rows/pallas_call | solution.py:136
  89.4 8.9 %all-to-all-start = ((bf16[32,8,4096]{2,1,0:T(8,128)(2,1)}), bf16[32,8,4096]{2,1,0:T(8,128)(2,1)}, u32[]{:S(2)}, u32[]{:S(2)}) async-start(bf16[32,8,4096]{2,1,0:T(8,128)(2,1)} %bitcast.11), calls=%async_computation | async-start | bytes 4194304 | tf_op jit(solution)/shard_map/all_to_all | solution.py:362
  98.4 0.2 fusion.7
  98.6 0.2 fusion.6
  98.8 0.1 multiply_add_fusion
  98.8 0.1 iota_compare_fusion.3
  98.9 0.7 collective-permute-start.17
  99.6 0.7 collective-permute-start.19
  100.3 0.7 collective-permute-start.21
  101.0 0.9 collective-permute-start.23
  101.9 0.1 iota_compare_fusion.4
  102.0 0.7 add_convert_fusion.rows_ref
  102.8 2.1 %total.1 = f32[2,4,64,1024]{3,2,1,0:T(8,128)} custom-call(s32[3]{0:T(128)S(1)} %pad_add_fusion.1.place_ref, f32[2,4,64,1024]{3,2,1,0:T(8,128)S(1)} %copy-done.1, bf16[2,64,1024]{2,1,0:T(8,128)(2,1)S(1)} %collective-permute-done.17.refs_0_, bf16[2,64,1024]{2,1,0:T(8,128)(2,1)S(1)} %collective-permute-done.19.refs_1_, ...), custom_call_target="tpu_custom_call" | custom-call | flops 524288 | bytes 5242880 | tf_op jit(solution)/shard_map/total/pallas_call | solution.py:241
  104.9 44.0 %all-to-all-done = bf16[32,8,4096]{2,1,0:T(8,128)(2,1)} async-done(((bf16[32,8,4096]{2,1,0:T(8,128)(2,1)}), bf16[32,8,4096]{2,1,0:T(8,128)(2,1)}, u32[]{:S(2)}, u32[]{:S(2)}) %all-to-all-start) | async-done | bytes 2097184 | tf_op jit(solution)/shard_map/all_to_all | solution.py:362
  148.9 7.2 %place_rows.1 = (f32[2,256,1024]{2,1,0:T(8,128)}, f32[2,256,1024]{2,1,0:T(8,128)}) custom-call(s32[2,1024]{1,0:T(2,128)} %maps_ref.1, bf16[2,256,256]{2,1,0:T(8,128)(2,1)} %add_convert_fusion.rows_ref, bf16[256,4096]{1,0:T(8,128)(2,1)} %bitcast.12.received, f32[2,256,1024]{2,1,0:T(8,128)} %bitcast.49, f32[2,256,1024]{2,1,0:T(8,128)} %bitcast.50), custom_call_target="tpu_custom_call" | custom-call | flops 2684354560 | bytes 8388608 | tf_op jit(solution)/shard_map/place_rows/pallas_call | solution.py:196
  (33 shorter events, 0.2 us)
Async XLA Ops:
  0.6 0.8 copy-start
  0.6 9.8 %copy-start.2 = (s32[2,8,1024]{2,1,0:T(8,128)S(1)}, s32[2,8,1024]{2,1,0:T(8,128)}, u32[]{:S(2)}) copy-start(s32[2,8,1024]{2,1,0:T(8,128)} %param.10) | copy-start | bytes 196612
  1.4 14.2 %collective-permute-start = (f32[2,1024]{1,0:T(2,128)S(1)}, f32[2,1024]{1,0:T(2,128)S(1)}, u32[]{:S(2)}, u32[]{:S(2)}) collective-permute-start(f32[2,1024]{1,0:T(2,128)S(1)} %bitcast.48), channel_id=1, source_target_pairs={{0,16},{1,17},{2,18},{3,19},{4,20},{5,21},{6,22},{7,23},{8,24},{9,... | collective-permute-start | bytes 24584 | tf_op jit(solution)/shard_map/ppermute | solution.py:282
  3.2 8.8 %collective-permute-start.1 = (bf16[2,64,1024]{2,1,0:T(8,128)(2,1)S(1)}, bf16[2,64,1024]{2,1,0:T(8,128)(2,1)S(1)}, u32[]{:S(2)}, u32[]{:S(2)}) collective-permute-start(bf16[2,64,1024]{2,1,0:T(8,128)(2,1)S(1)} %get-tuple-element.10), channel_id=1, source_target_pairs={{0,0},{1,1},{2,16},{3,17},{4,4},{5,5},{6,20},{7,21},{8,8},{9,9},{1... | collective-permute-start | bytes 786440 | tf_op jit(solution)/shard_map/ppermute | solution.py:282
  5.2 13.0 %collective-permute-start.5 = (bf16[2,64,1024]{2,1,0:T(8,128)(2,1)S(1)}, bf16[2,64,1024]{2,1,0:T(8,128)(2,1)S(1)}, u32[]{:S(2)}, u32[]{:S(2)}) collective-permute-start(bf16[2,64,1024]{2,1,0:T(8,128)(2,1)S(1)} %get-tuple-element.20), channel_id=1, source_target_pairs={{0,4},{1,5},{2,20},{3,21},{4,0},{5,1},{6,16},{7,17},{8,12},{9,13},... | collective-permute-start | bytes 786440 | tf_op jit(solution)/shard_map/ppermute | solution.py:282
  7.9 11.7 %collective-permute-start.9 = (bf16[2,64,1024]{2,1,0:T(8,128)(2,1)S(1)}, bf16[2,64,1024]{2,1,0:T(8,128)(2,1)S(1)}, u32[]{:S(2)}, u32[]{:S(2)}) collective-permute-start(bf16[2,64,1024]{2,1,0:T(8,128)(2,1)S(1)} %get-tuple-element.19), channel_id=1, source_target_pairs={{0,8},{1,9},{2,24},{3,25},{4,12},{5,13},{6,28},{7,29},{8,0},{9,1},... | collective-permute-start | bytes 786440 | tf_op jit(solution)/shard_map/ppermute | solution.py:282
  10.5 16.2 %collective-permute-start.13 = (bf16[2,64,1024]{2,1,0:T(8,128)(2,1)S(1)}, bf16[2,64,1024]{2,1,0:T(8,128)(2,1)S(1)}, u32[]{:S(2)}, u32[]{:S(2)}) collective-permute-start(bf16[2,64,1024]{2,1,0:T(8,128)(2,1)S(1)} %get-tuple-element.12), channel_id=1, source_target_pairs={{0,12},{1,13},{2,28},{3,29},{4,8},{5,9},{6,24},{7,25},{8,4},{9,5},... | collective-permute-start | bytes 786440 | tf_op jit(solution)/shard_map/ppermute | solution.py:282
  12.1 21.2 %collective-permute-start.2 = (bf16[2,64,1024]{2,1,0:T(8,128)(2,1)S(1)}, bf16[2,64,1024]{2,1,0:T(8,128)(2,1)S(1)}, u32[]{:S(2)}, u32[]{:S(2)}) collective-permute-start(bf16[2,64,1024]{2,1,0:T(8,128)(2,1)S(1)} %collective-permute-done.1.refs_0_), channel_id=1, source_target_pairs={{0,16},{1,17},{2,18},{3,19},{4,20},{5,21},{6,22},{7,23},{8,24},{9,... | collective-permute-start | bytes 786440 | tf_op jit(solution)/shard_map/ppermute | solution.py:282
  15.6 18.2 %collective-permute-start.3 = (bf16[2,64,1024]{2,1,0:T(8,128)(2,1)S(1)}, bf16[2,64,1024]{2,1,0:T(8,128)(2,1)S(1)}, u32[]{:S(2)}, u32[]{:S(2)}) collective-permute-start(bf16[2,64,1024]{2,1,0:T(8,128)(2,1)S(1)} %collective-permute-done.1.refs_0_), channel_id=1, source_target_pairs={{0,1},{1,0},{2,3},{3,2},{4,5},{5,4},{6,7},{7,6},{8,9},{9,8},{10,11... | collective-permute-start | bytes 786440 | tf_op jit(solution)/shard_map/ppermute | solution.py:282
  18.2 17.2 %collective-permute-start.6 = (bf16[2,64,1024]{2,1,0:T(8,128)(2,1)S(1)}, bf16[2,64,1024]{2,1,0:T(8,128)(2,1)S(1)}, u32[]{:S(2)}, u32[]{:S(2)}) collective-permute-start(bf16[2,64,1024]{2,1,0:T(8,128)(2,1)S(1)} %collective-permute-done.5.refs_4_), channel_id=1, source_target_pairs={{0,16},{1,17},{2,18},{3,19},{4,20},{5,21},{6,22},{7,23},{8,24},{9,... | collective-permute-start | bytes 786440 | tf_op jit(solution)/shard_map/ppermute | solution.py:282
  19.6 16.0 %collective-permute-start.7 = (bf16[2,64,1024]{2,1,0:T(8,128)(2,1)S(1)}, bf16[2,64,1024]{2,1,0:T(8,128)(2,1)S(1)}, u32[]{:S(2)}, u32[]{:S(2)}) collective-permute-start(bf16[2,64,1024]{2,1,0:T(8,128)(2,1)S(1)} %collective-permute-done.5.refs_4_), channel_id=1, source_target_pairs={{0,1},{1,0},{2,3},{3,2},{4,5},{5,4},{6,7},{7,6},{8,9},{9,8},{10,11... | collective-permute-start | bytes 786440 | tf_op jit(solution)/shard_map/ppermute | solution.py:282
  26.6 11.5 %collective-permute-start.10 = (bf16[2,64,1024]{2,1,0:T(8,128)(2,1)S(1)}, bf16[2,64,1024]{2,1,0:T(8,128)(2,1)S(1)}, u32[]{:S(2)}, u32[]{:S(2)}) collective-permute-start(bf16[2,64,1024]{2,1,0:T(8,128)(2,1)S(1)} %collective-permute-done.9.refs_8_), channel_id=1, source_target_pairs={{0,16},{1,17},{2,18},{3,19},{4,20},{5,21},{6,22},{7,23},{8,24},{9,... | collective-permute-start | bytes 786440 | tf_op jit(solution)/shard_map/ppermute | solution.py:282
  33.3 9.2 %collective-permute-start.11 = (bf16[2,64,1024]{2,1,0:T(8,128)(2,1)S(1)}, bf16[2,64,1024]{2,1,0:T(8,128)(2,1)S(1)}, u32[]{:S(2)}, u32[]{:S(2)}) collective-permute-start(bf16[2,64,1024]{2,1,0:T(8,128)(2,1)S(1)} %collective-permute-done.9.refs_8_), channel_id=1, source_target_pairs={{0,1},{1,0},{2,3},{3,2},{4,5},{5,4},{6,7},{7,6},{8,9},{9,8},{10,11... | collective-permute-start | bytes 786440 | tf_op jit(solution)/shard_map/ppermute | solution.py:282
  33.8 14.3 %collective-permute-start.15 = (bf16[2,64,1024]{2,1,0:T(8,128)(2,1)S(1)}, bf16[2,64,1024]{2,1,0:T(8,128)(2,1)S(1)}, u32[]{:S(2)}, u32[]{:S(2)}) collective-permute-start(bf16[2,64,1024]{2,1,0:T(8,128)(2,1)S(1)} %collective-permute-done.13.refs_12_), channel_id=1, source_target_pairs={{0,1},{1,0},{2,3},{3,2},{4,5},{5,4},{6,7},{7,6},{8,9},{9,8},{10,11... | collective-permute-start | bytes 786440 | tf_op jit(solution)/shard_map/ppermute | solution.py:282
  35.5 13.1 %collective-permute-start.14 = (bf16[2,64,1024]{2,1,0:T(8,128)(2,1)S(1)}, bf16[2,64,1024]{2,1,0:T(8,128)(2,1)}, u32[]{:S(2)}, u32[]{:S(2)}) collective-permute-start(bf16[2,64,1024]{2,1,0:T(8,128)(2,1)S(1)} %collective-permute-done.13.refs_12_), channel_id=1, source_target_pairs={{0,16},{1,17},{2,18},{3,19},{4,20},{5,21},{6,22},{7,23},{8,24},{9,... | collective-permute-start | bytes 786440 | tf_op jit(solution)/shard_map/ppermute | solution.py:282
  35.6 13.1 %collective-permute-start.4 = (bf16[2,64,1024]{2,1,0:T(8,128)(2,1)S(1)}, bf16[2,64,1024]{2,1,0:T(8,128)(2,1)}, u32[]{:S(2)}, u32[]{:S(2)}) collective-permute-start(bf16[2,64,1024]{2,1,0:T(8,128)(2,1)S(1)} %collective-permute-done.3.refs_2_), channel_id=1, source_target_pairs={{0,16},{1,17},{2,18},{3,19},{4,20},{5,21},{6,22},{7,23},{8,24},{9,... | collective-permute-start | bytes 786440 | tf_op jit(solution)/shard_map/ppermute | solution.py:282
  38.2 10.4 %collective-permute-start.8 = (bf16[2,64,1024]{2,1,0:T(8,128)(2,1)S(1)}, bf16[2,64,1024]{2,1,0:T(8,128)(2,1)}, u32[]{:S(2)}, u32[]{:S(2)}) collective-permute-start(bf16[2,64,1024]{2,1,0:T(8,128)(2,1)S(1)} %collective-permute-done.7.refs_6_), channel_id=1, source_target_pairs={{0,16},{1,17},{2,18},{3,19},{4,20},{5,21},{6,22},{7,23},{8,24},{9,... | collective-permute-start | bytes 786440 | tf_op jit(solution)/shard_map/ppermute | solution.py:282
  42.5 6.2 %collective-permute-start.12 = (bf16[2,64,1024]{2,1,0:T(8,128)(2,1)S(1)}, bf16[2,64,1024]{2,1,0:T(8,128)(2,1)}, u32[]{:S(2)}, u32[]{:S(2)}) collective-permute-start(bf16[2,64,1024]{2,1,0:T(8,128)(2,1)S(1)} %collective-permute-done.11.refs_10_), channel_id=1, source_target_pairs={{0,16},{1,17},{2,18},{3,19},{4,20},{5,21},{6,22},{7,23},{8,24},{9,... | collective-permute-start | bytes 786440 | tf_op jit(solution)/shard_map/ppermute | solution.py:282
  48.1 1.7 %collective-permute-start.16 = (bf16[2,64,1024]{2,1,0:T(8,128)(2,1)S(1)}, bf16[2,64,1024]{2,1,0:T(8,128)(2,1)}, u32[]{:S(2)}, u32[]{:S(2)}) collective-permute-start(bf16[2,64,1024]{2,1,0:T(8,128)(2,1)S(1)} %collective-permute-done.15.refs_14_), channel_id=1, source_target_pairs={{0,16},{1,17},{2,18},{3,19},{4,20},{5,21},{6,22},{7,23},{8,24},{9,... | collective-permute-start | bytes 786440 | tf_op jit(solution)/shard_map/ppermute | solution.py:282
  64.8 13.7 %collective-permute-start.18 = (bf16[2,64,1024]{2,1,0:T(8,128)(2,1)S(1)}, bf16[2,64,1024]{2,1,0:T(8,128)(2,1)S(1)}, u32[]{:S(2)}, u32[]{:S(2)}) collective-permute-start(bf16[2,64,1024]{2,1,0:T(8,128)(2,1)S(1)} %ladder.6), channel_id=1, source_target_pairs={{0,4},{1,5},{2,6},{3,7},{4,0},{5,1},{6,2},{7,3},{8,12},{9,13},{10,... | collective-permute-start | bytes 786440 | tf_op jit(solution)/shard_map/ppermute | solution.py:282
  66.0 21.3 %collective-permute-start.20 = (bf16[2,64,1024]{2,1,0:T(8,128)(2,1)S(1)}, bf16[2,64,1024]{2,1,0:T(8,128)(2,1)S(1)}, u32[]{:S(2)}, u32[]{:S(2)}) collective-permute-start(bf16[2,64,1024]{2,1,0:T(8,128)(2,1)S(1)} %ladder.7), channel_id=1, source_target_pairs={{0,8},{1,9},{2,10},{3,11},{4,12},{5,13},{6,14},{7,15},{8,0},{9,1},... | collective-permute-start | bytes 786440 | tf_op jit(solution)/shard_map/ppermute | solution.py:282
  67.4 20.0 %collective-permute-start.22 = (bf16[2,64,1024]{2,1,0:T(8,128)(2,1)S(1)}, bf16[2,64,1024]{2,1,0:T(8,128)(2,1)S(1)}, u32[]{:S(2)}, u32[]{:S(2)}) collective-permute-start(bf16[2,64,1024]{2,1,0:T(8,128)(2,1)S(1)} %get-tuple-element.14), channel_id=1, source_target_pairs={{0,12},{1,13},{2,14},{3,15},{4,8},{5,9},{6,10},{7,11},{8,4},{9,5},... | collective-permute-start | bytes 786440 | tf_op jit(solution)/shard_map/ppermute | solution.py:282
  89.4 13.4 %copy-start.1 = (f32[2,4,64,1024]{3,2,1,0:T(8,128)S(1)}, f32[2,4,64,1024]{3,2,1,0:T(8,128)}, u32[]{:S(2)}) copy-start(f32[2,4,64,1024]{3,2,1,0:T(8,128)} %vertex.1) | copy-start | bytes 6291460
  89.4 59.5 %all-to-all-start = ((bf16[32,8,4096]{2,1,0:T(8,128)(2,1)}), bf16[32,8,4096]{2,1,0:T(8,128)(2,1)}, u32[]{:S(2)}, u32[]{:S(2)}) async-start(bf16[32,8,4096]{2,1,0:T(8,128)(2,1)} %bitcast.11), calls=%async_computation | async-start | bytes 4194304 | tf_op jit(solution)/shard_map/all_to_all | solution.py:362
  98.9 3.8 %collective-permute-start.17 = (bf16[2,64,1024]{2,1,0:T(8,128)(2,1)S(1)}, bf16[2,64,1024]{2,1,0:T(8,128)(2,1)S(1)}, u32[]{:S(2)}, u32[]{:S(2)}) collective-permute-start(bf16[2,64,1024]{2,1,0:T(8,128)(2,1)S(1)} %ladder.5.refs_0_), channel_id=1, source_target_pairs={{0,0},{1,1},{2,16},{3,17},{4,4},{5,5},{6,20},{7,21},{8,8},{9,9},{1... | collective-permute-start | bytes 786440 | tf_op jit(solution)/shard_map/ppermute | solution.py:282
  99.6 3.1 %collective-permute-start.19 = (bf16[2,64,1024]{2,1,0:T(8,128)(2,1)S(1)}, bf16[2,64,1024]{2,1,0:T(8,128)(2,1)S(1)}, u32[]{:S(2)}, u32[]{:S(2)}) collective-permute-start(bf16[2,64,1024]{2,1,0:T(8,128)(2,1)S(1)} %collective-permute-done.18.refs_1_), channel_id=1, source_target_pairs={{0,0},{1,1},{2,16},{3,17},{4,4},{5,5},{6,20},{7,21},{8,8},{9,9},{1... | collective-permute-start | bytes 786440 | tf_op jit(solution)/shard_map/ppermute | solution.py:282
  100.3 2.4 %collective-permute-start.21 = (bf16[2,64,1024]{2,1,0:T(8,128)(2,1)S(1)}, bf16[2,64,1024]{2,1,0:T(8,128)(2,1)S(1)}, u32[]{:S(2)}, u32[]{:S(2)}) collective-permute-start(bf16[2,64,1024]{2,1,0:T(8,128)(2,1)S(1)} %collective-permute-done.20.refs_2_), channel_id=1, source_target_pairs={{0,0},{1,1},{2,16},{3,17},{4,4},{5,5},{6,20},{7,21},{8,8},{9,9},{1... | collective-permute-start | bytes 786440 | tf_op jit(solution)/shard_map/ppermute | solution.py:282
  101.0 1.8 %collective-permute-start.23 = (bf16[2,64,1024]{2,1,0:T(8,128)(2,1)S(1)}, bf16[2,64,1024]{2,1,0:T(8,128)(2,1)S(1)}, u32[]{:S(2)}, u32[]{:S(2)}) collective-permute-start(bf16[2,64,1024]{2,1,0:T(8,128)(2,1)S(1)} %collective-permute-done.22.refs_3_), channel_id=1, source_target_pairs={{0,0},{1,1},{2,16},{3,17},{4,4},{5,5},{6,20},{7,21},{8,8},{9,9},{1... | collective-permute-start | bytes 786440 | tf_op jit(solution)/shard_map/ppermute | solution.py:282
